TPU v7x, 256 devices: a whole 4x4x8 slice. The times are simulated.
256 devices in a mesh: dp: 8 (over z_hi, y), seq: 32 (over x, z_lo, core).
Axes of the slice: x: 4, y: 4, z: 8 (z_hi: 2, z_lo: 4; z = z_hi * 4 + z_lo), core: 2. Of those that a mesh axis runs over, the one named last changes fastest.
Arguments:
- patches: bfloat16 [8, 4096, 2048], P('dp', 'seq'), may hold values from -6 to 6
- key_proj: bfloat16 [8, 4096, 128], P('dp', 'seq'), may hold values from -6 to 6
- query_proj: bfloat16 [8, 4096, 128], P('dp', 'seq'), may hold values from -6 to 6
- step_raw: float32 [8, 32, 4096], P('dp', None, 'seq'), may hold values from -16 to -1
- log_decay: float32 [2, 32], replicated, may hold values from -0.7 to 0.7
- step_bias: float32 [2, 32], replicated, may hold values from -0.5 to 0.5
- skip_gain: float32 [32], replicated, may hold values from 0.5 to 1.5
- group_valid: int32 [8, 32], P('dp', 'seq'), may hold values 0 or 1
- out_grad: bfloat16 [8, 4096, 2048], P('dp', 'seq'), may hold values from -6 to 6
Outputs:
- output: bfloat16 [8, 4096, 2048], P('dp', 'seq')
- patch_grad: bfloat16 [8, 4096, 2048], P('dp', 'seq')
- key_grad: float32 [8, 4096, 128], P('dp', 'seq')
- query_grad: float32 [8, 4096, 128], P('dp', 'seq')
- step_grad: float32 [8, 32, 4096], P('dp', None, 'seq')
- decay_grad: float32 [2, 32], replicated
- bias_grad: float32 [2, 32], replicated
- skip_grad: float32 [32], replicated
All inputs are finite; a program needn't handle non-finite values. No bound on the sum of `group_valid` on one device may be relied on, other than what follows from the above.
Results may differ from a plain program's by a relative error of at most 0.0037.
Values may be sent and summed in bfloat16 or wider, within the bound.
A program may use at most 320 MiB of HBM per device.

v0:
```python
import jax
import jax.numpy as jnp
from jax import lax
from jax.sharding import PartitionSpec as P

GROUP = 128


highest = lax.Precision.HIGHEST


def entering_2(part, axis, combine, identity, reverse):
    count = lax.axis_size(axis)
    place = lax.axis_index(axis)
    ahead = count - 1 - place if reverse else place
    gathered = jax.tree.map(lambda a: lax.all_gather(a, axis), part)
    state = jax.tree.map(lambda a, e: jnp.zeros_like(a) + jnp.asarray(e, a.dtype), part, identity)

    def one(lap, state):
        source = count - 1 - lap if reverse else lap
        return combine(
            state, jax.tree.map(lambda a: lax.dynamic_index_in_dim(a, source, 0, False), gathered)
        )

    return lax.fori_loop(0, ahead, one, state)


def partner(block, axis, bit):
    count = lax.axis_size(axis)
    route = []
    for low in range(count):
        high = low | 1 << bit
        if high != low and high < count:
            route += [(low, high), (high, low)]
    return lax.ppermute(block, axis, route)


def cumulative_decay(step_rows, decay_rate):
    return jnp.cumsum(step_rows * decay_rate[None, :, None], axis=2)


def group_states(inputs, key_rows, step_rows, decay_rate):
    cumulative = cumulative_decay(step_rows, decay_rate)
    to_end = jnp.exp(cumulative[:, :, -1:] - cumulative) * step_rows
    weighted = inputs * jnp.transpose(to_end, (0, 2, 1))[:, :, :, None]
    states = jnp.einsum("kqhp,kqn->khpn", weighted, key_rows, precision=highest)
    return (cumulative[:, :, -1], states)


def run_groups(log_group, states, start_state):

    def advance(running, pieces):
        log_piece, state_piece = pieces
        return (jnp.exp(log_piece)[:, None, None] * running + state_piece, running)

    final_state, entering = lax.scan(advance, start_state, (log_group, states))
    return (entering, final_state)


def enter_states(log_group, states, start_state):
    return run_groups(log_group, states, start_state)[0]


def device_total(log_group, states):
    total_decay = jnp.exp(jnp.sum(log_group, axis=0))
    return (total_decay, run_groups(log_group, states, jnp.zeros_like(states[0]))[1])


def group_outputs(inputs, key_rows, query_rows, step_rows, decay_rate, entering):
    cumulative = cumulative_decay(step_rows, decay_rate)
    length = cumulative.shape[2]
    causal = jnp.arange(length)[:, None] >= jnp.arange(length)[None, :]
    spread = cumulative[:, :, :, None] - cumulative[:, :, None, :]
    within = jnp.where(causal, jnp.exp(jnp.where(causal, spread, 0.0)), 0.0)
    scores = jnp.einsum("kqn,ksn->kqs", query_rows, key_rows, precision=highest)
    mixing = within * scores[:, None, :, :]
    driven = inputs * jnp.transpose(step_rows, (0, 2, 1))[:, :, :, None]
    inside = jnp.einsum("khqs,kshp->kqhp", mixing, driven, precision=highest)
    carried = jnp.einsum("kqn,khpn->kqhp", query_rows, entering, precision=highest)
    return inside + carried * jnp.transpose(jnp.exp(cumulative), (0, 2, 1))[:, :, :, None]


def scan_join(earlier, later):
    return (earlier[0] * later[0], later[0][:, None, None] * earlier[1] + later[1])


def branch_pass(
    inputs, key_rows, query_rows, step_rows, decay_rate, cotangent, scan_states, scan_back
):
    (log_group, states), back_groups = jax.vjp(
        group_states, inputs, key_rows, step_rows, decay_rate
    )
    (total_decay, total_state), back_total = jax.vjp(device_total, log_group, states)
    start_state = scan_states(total_decay, total_state)
    entering, back_enter = jax.vjp(enter_states, log_group, states, start_state)
    outputs, back_outputs = jax.vjp(
        group_outputs, inputs, key_rows, query_rows, step_rows, decay_rate, entering
    )
    grad_in, grad_key, grad_query, grad_step, grad_rate, grad_enter = back_outputs(cotangent)
    grad_log, grad_states, grad_start = back_enter(grad_enter)
    arriving = scan_back(total_decay, grad_start)
    grad_decay = jnp.sum(arriving * start_state, axis=(1, 2))
    grad_log_total, grad_states_total = back_total((grad_decay, arriving))
    more_in, more_key, more_step, more_rate = back_groups(
        (grad_log + grad_log_total, grad_states + grad_states_total)
    )
    return (
        outputs,
        grad_in + more_in,
        grad_key + more_key,
        grad_query,
        grad_step + more_step,
        grad_rate + more_rate,
    )


def run_branch(
    patch_rows,
    key_rows,
    query_rows,
    raw_steps,
    token_mask,
    bias_row,
    decay_row,
    out_rows,
    scan_states,
    scan_back,
):
    rows_total, feat_width = patch_rows.shape
    head_count = raw_steps.shape[0]
    block_count = rows_total // GROUP
    head_dim = feat_width // head_count
    inputs = patch_rows.astype(jnp.float32).reshape(block_count, GROUP, head_count, head_dim)
    keyed = key_rows.astype(jnp.float32).reshape(block_count, GROUP, -1)
    queried = query_rows.astype(jnp.float32).reshape(block_count, GROUP, -1)
    shifted = raw_steps + bias_row[:, None]
    slopes = jax.nn.sigmoid(shifted) * token_mask[None, :]
    step_rows = (
        (jax.nn.softplus(shifted) * token_mask[None, :])
        .reshape(head_count, block_count, GROUP)
        .transpose(1, 0, 2)
    )
    decay_rate = -jnp.exp(decay_row)
    cotangent = (out_rows.astype(jnp.float32) * token_mask[:, None]).reshape(
        block_count, GROUP, head_count, head_dim
    )
    outputs, grad_in, grad_key, grad_query, grad_step, grad_rate = branch_pass(
        inputs, keyed, queried, step_rows, decay_rate, cotangent, scan_states, scan_back
    )
    raw_grad = grad_step.transpose(1, 0, 2).reshape(head_count, rows_total) * slopes
    return (
        outputs.reshape(rows_total, feat_width),
        grad_in.reshape(rows_total, feat_width),
        grad_key.reshape(rows_total, -1),
        grad_query.reshape(rows_total, -1),
        raw_grad,
        grad_rate * decay_rate,
        jnp.sum(raw_grad, axis=1),
    )


def body(
    patches, key_proj, query_proj, step_raw, log_decay, step_bias, skip_gain, group_valid, out_grad
):
    head_count = step_raw.shape[1]
    token_mask = jnp.repeat(group_valid[0].astype(jnp.float32), GROUP)

    def forward_states(decays, states):
        return entering_2(
            (decays, states),
            "seq",
            scan_join,
            (jnp.ones_like(decays), jnp.zeros_like(states)),
            False,
        )[1]

    def forward_back(decays, states):
        return entering_2(
            (decays, states),
            "seq",
            scan_join,
            (jnp.ones_like(decays), jnp.zeros_like(states)),
            True,
        )[1]

    fwd = run_branch(
        patches[0],
        key_proj[0],
        query_proj[0],
        step_raw[0],
        token_mask,
        step_bias[0],
        log_decay[0],
        out_grad[0],
        forward_states,
        forward_back,
    )

    def mirrored_states(decays, states):
        return entering_2(
            (decays, states),
            "seq",
            scan_join,
            (jnp.ones_like(decays), jnp.zeros_like(states)),
            False,
        )[1]

    def mirrored_back(decays, states):
        return entering_2(
            (decays, states),
            "seq",
            scan_join,
            (jnp.ones_like(decays), jnp.zeros_like(states)),
            True,
        )[1]

    level_count = lax.axis_size("seq").bit_length() - 1
    moved = (patches[0], key_proj[0], query_proj[0], out_grad[0])
    timing = (step_raw[0], token_mask)
    for which_bit in range(level_count):
        moved = partner((moved[0], moved[1], moved[2], moved[3]), "seq", which_bit)
        timing = partner((timing[0], timing[1]), "seq", which_bit)
    rev = run_branch(
        moved[0][::-1],
        moved[1][::-1],
        moved[2][::-1],
        timing[0][:, ::-1],
        timing[1][::-1],
        step_bias[1],
        log_decay[1],
        moved[3][::-1],
        mirrored_states,
        mirrored_back,
    )
    sending = (rev[0][::-1].astype(jnp.bfloat16), rev[1][::-1].astype(jnp.bfloat16))
    returning = (rev[2][::-1], rev[3][::-1], rev[4][:, ::-1])
    for which_bit in range(level_count):
        sending = partner((sending[0], sending[1]), "seq", which_bit)
        returning = partner((returning[0], returning[1], returning[2]), "seq", which_bit)
    rev_output = sending[0].astype(jnp.float32)
    rev_patch = sending[1].astype(jnp.float32)
    rev_key, rev_query, rev_step = returning
    patch_wide = patches[0].astype(jnp.float32)
    rows_total, feat_width = patch_wide.shape
    head_dim = feat_width // head_count
    skip_wide = jnp.repeat(skip_gain, head_dim)
    cotangent = out_grad[0].astype(jnp.float32) * token_mask[:, None]
    output = (token_mask[:, None] * (fwd[0] + rev_output + skip_wide[None, :] * patch_wide)).astype(
        jnp.bfloat16
    )
    patch_grad = (fwd[1] + rev_patch + skip_wide[None, :] * cotangent).astype(jnp.bfloat16)
    key_grad = fwd[2] + rev_key
    query_grad = fwd[3] + rev_query
    step_grad = fwd[4] + rev_step
    skip_term = jnp.sum(
        (cotangent * patch_wide).reshape(rows_total, head_count, head_dim), axis=(0, 2)
    )
    decay_grad, bias_grad, skip_grad = lax.psum(
        (jnp.stack([fwd[5], rev[5]]), jnp.stack([fwd[6], rev[6]]), skip_term), ("dp", "seq")
    )
    return (
        output[None],
        patch_grad[None],
        key_grad[None],
        query_grad[None],
        step_grad[None],
        decay_grad,
        bias_grad,
        skip_grad,
    )


def solution(mesh):
    in_specs = (
        P("dp", "seq", None),
        P("dp", "seq", None),
        P("dp", "seq", None),
        P("dp", None, "seq"),
        P(),
        P(),
        P(),
        P("dp", "seq"),
        P("dp", "seq", None),
    )
    out_specs = (
        P("dp", "seq", None),
        P("dp", "seq", None),
        P("dp", "seq", None),
        P("dp", "seq", None),
        P("dp", None, "seq"),
        P(),
        P(),
        P(),
    )
    return jax.shard_map(body, mesh=mesh, in_specs=in_specs, out_specs=out_specs, check_vma=False)
```

profile of v0, /device:TPU:1, one launch (start us, length us, event | category | flops | bytes accessed | tf_op | source)
XLA Modules:
  0.0 1103.9 jit_solution(2400996692749344397)
XLA Ops:
  23.2 15.0 %collective-permute-done.1 = bf16[128,2048]{0,1:T(8,128)(2,1)S(1)} collective-permute-done((bf16[128,2048]{0,1:T(8,128)(2,1)S(1)}, bf16[128,2048]{0,1:T(8,128)(2,1)S(1)}, u32[]{:S(2)}, u32[]{:S(2)}) %collective-permute-start.1) | collective-permute-done | bytes 524320 | tf_op jit(solution)/shard_map/ppermute | solution.py:35
  39.2 35.6 %collective-permute-done.2 = bf16[128,2048]{0,1:T(8,128)(2,1)S(1)} collective-permute-done((bf16[128,2048]{0,1:T(8,128)(2,1)S(1)}, bf16[128,2048]{0,1:T(8,128)(2,1)S(1)}, u32[]{:S(2)}, u32[]{:S(2)}) %collective-permute-start.2) | collective-permute-done | bytes 524320 | tf_op jit(solution)/shard_map/ppermute | solution.py:35
  91.4 8.1 collective-permute-done.8
  127.6 21.2 %collective-permute-done.23 = bf16[128,128]{1,0:T(8,128)(2,1)S(1)} collective-permute-done((bf16[128,128]{1,0:T(8,128)(2,1)S(1)}, bf16[128,128]{1,0:T(8,128)(2,1)S(1)}, u32[]{:S(2)}, u32[]{:S(2)}) %collective-permute-start.23) | collective-permute-done | bytes 32800 | tf_op jit(solution)/shard_map/ppermute | solution.py:35
  158.1 6.2 collective-permute-start.30
  166.0 24.8 %collective-permute-done.31 = bf16[128,2048]{0,1:T(8,128)(2,1)S(1)} collective-permute-done((bf16[128,2048]{0,1:T(8,128)(2,1)S(1)}, bf16[128,2048]{0,1:T(8,128)(2,1)S(1)}, u32[]{:S(2)}, u32[]{:S(2)}) %collective-permute-start.31) | collective-permute-done | bytes 524320 | tf_op jit(solution)/shard_map/ppermute | solution.py:35
  190.9 36.9 %collective-permute-done.32 = bf16[128,2048]{0,1:T(8,128)(2,1)S(1)} collective-permute-done((bf16[128,2048]{0,1:T(8,128)(2,1)S(1)}, bf16[128,2048]{0,1:T(8,128)(2,1)S(1)}, u32[]{:S(2)}, u32[]{:S(2)}) %collective-permute-start.32) | collective-permute-done | bytes 524320 | tf_op jit(solution)/shard_map/ppermute | solution.py:35
  227.8 20.7 %collective-permute-done.33 = bf16[128,2048]{0,1:T(8,128)(2,1)} collective-permute-done((bf16[128,2048]{0,1:T(8,128)(2,1)S(1)}, bf16[128,2048]{0,1:T(8,128)(2,1)}, u32[]{:S(2)}, u32[]{:S(2)}) %collective-permute-start.33) | collective-permute-done | bytes 524320 | tf_op jit(solution)/shard_map/ppermute | solution.py:35
  280.0 48.1 %all-gather = f32[32,32,1]{1,2,0:T(1,128)} all-gather(f32[1,32,1]{1,2,0:T(1,128)} %get-tuple-element.570), channel_id=2, replica_groups=mesh['dp'=8,'seq'=32] {'seq'}, dimensions={0}, use_global_device_ids=true | all-gather | bytes 4224 | tf_op jit(solution)/shard_map/all_gather | solution.py:16
  339.0 41.3 %all-gather.2 = f32[32,32,1]{1,2,0:T(1,128)} all-gather(f32[1,32,1]{1,2,0:T(1,128)} %get-tuple-element.568), channel_id=4, replica_groups=mesh['dp'=8,'seq'=32] {'seq'}, dimensions={0}, use_global_device_ids=true | all-gather | bytes 4224 | tf_op jit(solution)/shard_map/all_gather | solution.py:16
  381.6 8.8 fusion.33
  395.5 65.3 %while.34 = (s32[]{:T(128)}, f32[32,64,128]{2,1,0:T(8,128)S(1)}, s32[]{:T(128)}, f32[32,32]{1,0:T(8,128)}, f32[32,32,64,128]{3,2,1,0:T(8,128)}, /*index=5*/s32[]{:T(128)}, s32[]{:T(128)}, s32[]{:T(128)}, s32[]{:T(128)}) while((s32[]{:T(128)}, f32[32,64,128]{2,1,0:T(8,128)S(1)}, s32[]{:T(128)}, f32[32,32]{1,0:T(8,128)}, ...), condition=%wide.region_7.8_spmd, body=%wide.region_6.7_spmd.sunk | while | flops 524294 | bytes 3146267 | solution.py:25
  492.3 5.3 fusion.27
  497.5 136.7 %all-gather.13.cloned.1.call-done = f32[1024,64,128]{2,1,0:T(8,128)} async-done(((f32[32,64,128]{2,1,0:T(8,128)}), f32[1024,64,128]{2,1,0:T(8,128)}) %all-gather.13.cloned.1.call-update) | async-done | bytes 33554448 | tf_op jit(solution)/shard_map/all_gather | solution.py:16
  642.4 5.6 rev.38
  648.0 172.9 %all-gather.17.cloned.1.call-done = f32[1024,64,128]{2,1,0:T(8,128)} async-done(((f32[32,64,128]{2,1,0:T(8,128)}), f32[1024,64,128]{2,1,0:T(8,128)}) %all-gather.17.cloned.1.call-update) | async-done | bytes 33554448 | tf_op jit(solution)/shard_map/all_gather | solution.py:16
  821.0 64.6 %while.35 = (s32[]{:T(128)}, f32[32,64,128]{2,1,0:T(8,128)S(1)}, s32[]{:T(128)}, f32[32,32]{1,0:T(8,128)}, f32[32,32,64,128]{3,2,1,0:T(8,128)}, /*index=5*/s32[]{:T(128)}, s32[]{:T(128)}, s32[]{:T(128)}, s32[]{:T(128)}) while((s32[]{:T(128)}, f32[32,64,128]{2,1,0:T(8,128)S(1)}, s32[]{:T(128)}, f32[32,32]{1,0:T(8,128)}, ...), condition=%wide.region_9.10_spmd, body=%wide.region_8.9_spmd.sunk | while | flops 524294 | bytes 3146267 | solution.py:25
  888.6 8.7 rev.40
  917.2 12.5 %collective-permute-done.36 = bf16[128,2048]{0,1:T(8,128)(2,1)} collective-permute-done((bf16[128,2048]{0,1:T(8,128)(2,1)}, bf16[128,2048]{0,1:T(8,128)(2,1)}, u32[]{:S(2)}, u32[]{:S(2)}) %collective-permute-start.36) | collective-permute-done | bytes 524320 | tf_op jit(solution)/shard_map/ppermute | solution.py:35
  939.0 14.5 %collective-permute-done.27 = bf16[128,2048]{0,1:T(8,128)(2,1)} collective-permute-done((bf16[128,2048]{0,1:T(8,128)(2,1)}, bf16[128,2048]{0,1:T(8,128)(2,1)}, u32[]{:S(2)}, u32[]{:S(2)}) %collective-permute-start.27) | collective-permute-done | bytes 524320 | tf_op jit(solution)/shard_map/ppermute | solution.py:35
  953.5 11.2 %collective-permute-done.37 = bf16[128,2048]{0,1:T(8,128)(2,1)} collective-permute-done((bf16[128,2048]{0,1:T(8,128)(2,1)}, bf16[128,2048]{0,1:T(8,128)(2,1)}, u32[]{:S(2)}, u32[]{:S(2)}) %collective-permute-start.37) | collective-permute-done | bytes 524320 | tf_op jit(solution)/shard_map/ppermute | solution.py:35
  973.4 4.9 collective-permute-done.53
  979.4 81.9 %all-reduce.4 = (f32[2,32]{1,0:T(2,128)}, f32[2,32]{1,0:T(2,128)}, f32[32]{0:T(128)}) all-reduce(f32[2,32]{1,0:T(2,128)S(1)} %pad_maximum_fusion, f32[2,32]{1,0:T(2,128)S(1)} %pad_maximum_fusion.1, f32[32]{0:T(128)} %reduce_sum.392), channel_id=1, replica_groups=mesh['dp'=8,'seq'=32] {'dp','seq'}, use_global_device_ids=true, to_apply=%region_38.39 | all-reduce | flops 160 | bytes 1280 | tf_op jit(solution)/shard_map/psum | solution.py:258
  1069.7 20.9 %collective-permute-done.44 = f32[128,128]{1,0:T(8,128)S(1)} collective-permute-done((f32[128,128]{1,0:T(8,128)}, f32[128,128]{1,0:T(8,128)S(1)}, u32[]{:S(2)}, u32[]{:S(2)}) %collective-permute-start.44) | collective-permute-done | bytes 65568 | tf_op jit(solution)/shard_map/ppermute | solution.py:35
  (499 shorter events, 348.7 us)
Async XLA Ops:
  7.2 388.2 %all-gather.15.cloned.1.call-start = ((), (), s32[]{:S(2)}) async-start(), calls=%async_computation.2 | async-start | bytes 34603008 | tf_op jit(solution)/shard_map/all_gather | solution.py:16
  16.6 449.4 %all-gather.11.cloned.1.call-start = ((), (), s32[]{:S(2)}) async-start(), calls=%async_computation | async-start | bytes 34603008 | tf_op jit(solution)/shard_map/all_gather | solution.py:16
  18.3 615.9 %all-gather.13.cloned.1.call-start = ((), (), s32[]{:S(2)}) async-start(), calls=%async_computation.1 | async-start | bytes 34603008 | tf_op jit(solution)/shard_map/all_gather | solution.py:16
  38.2 36.7 %collective-permute-start.2 = (bf16[128,2048]{0,1:T(8,128)(2,1)S(1)}, bf16[128,2048]{0,1:T(8,128)(2,1)S(1)}, u32[]{:S(2)}, u32[]{:S(2)}) collective-permute-start(bf16[128,2048]{0,1:T(8,128)(2,1)S(1)} %collective-permute-done.1), channel_id=1, source_target_pairs={{0,4},{4,0},{1,5},{5,1},{2,6},{6,2},{3,7},{7,3},{8,12},{12,8},{9,1... | collective-permute-start | bytes 1572872 | tf_op jit(solution)/shard_map/ppermute | solution.py:35
  74.8 47.9 %collective-permute-start.3 = (bf16[128,2048]{0,1:T(8,128)(2,1)S(1)}, bf16[128,2048]{0,1:T(8,128)(2,1)S(1)}, u32[]{:S(2)}, u32[]{:S(2)}) collective-permute-start(bf16[128,2048]{0,1:T(8,128)(2,1)S(1)} %collective-permute-done.2), channel_id=1, source_target_pairs={{0,8},{8,0},{1,9},{9,1},{2,10},{10,2},{3,11},{11,3},{4,12},{12,4},... | collective-permute-start | bytes 1572872 | tf_op jit(solution)/shard_map/ppermute | solution.py:35
  85.3 34.2 %collective-permute-start.21 = (bf16[128,128]{1,0:T(8,128)(2,1)S(1)}, bf16[128,128]{1,0:T(8,128)(2,1)S(1)}, u32[]{:S(2)}, u32[]{:S(2)}) collective-permute-start(bf16[128,128]{1,0:T(8,128)(2,1)S(1)} %collective-permute-done.20), channel_id=1, source_target_pairs={{0,2},{2,0},{1,3},{3,1},{4,6},{6,4},{5,7},{7,5},{8,10},{10,8},{9,1... | collective-permute-start | bytes 98312 | tf_op jit(solution)/shard_map/ppermute | solution.py:35
  99.6 22.6 %collective-permute-start.9 = (f32[32,128]{0,1:T(8,128)S(1)}, f32[32,128]{0,1:T(8,128)S(1)}, u32[]{:S(2)}, u32[]{:S(2)}) collective-permute-start(f32[32,128]{0,1:T(8,128)S(1)} %collective-permute-done.8), channel_id=1, source_target_pairs={{0,16},{16,0},{1,17},{17,1},{2,18},{18,2},{3,19},{19,3},{4,20},{20... | collective-permute-start | bytes 49160 | tf_op jit(solution)/shard_map/ppermute | solution.py:35
  122.7 31.3 %collective-permute-start.4 = (bf16[128,2048]{0,1:T(8,128)(2,1)S(1)}, bf16[128,2048]{0,1:T(8,128)(2,1)S(1)}, u32[]{:S(2)}, u32[]{:S(2)}) collective-permute-start(bf16[128,2048]{0,1:T(8,128)(2,1)S(1)} %collective-permute-done.3), channel_id=1, source_target_pairs={{0,16},{16,0},{1,17},{17,1},{2,18},{18,2},{3,19},{19,3},{4,20},{20... | collective-permute-start | bytes 1572872 | tf_op jit(solution)/shard_map/ppermute | solution.py:35
  158.1 662.8 %all-gather.17.cloned.1.call-start = ((), (), s32[]{:S(2)}) async-start(), calls=%async_computation.3 | async-start | bytes 34603008 | tf_op jit(solution)/shard_map/all_gather | solution.py:16
  166.0 24.8 %collective-permute-start.31 = (bf16[128,2048]{0,1:T(8,128)(2,1)S(1)}, bf16[128,2048]{0,1:T(8,128)(2,1)S(1)}, u32[]{:S(2)}, u32[]{:S(2)}) collective-permute-start(bf16[128,2048]{0,1:T(8,128)(2,1)S(1)} %collective-permute-done.30), channel_id=1, source_target_pairs={{0,2},{2,0},{1,3},{3,1},{4,6},{6,4},{5,7},{7,5},{8,10},{10,8},{9,1... | collective-permute-start | bytes 1572872 | tf_op jit(solution)/shard_map/ppermute | solution.py:35
  190.9 37.0 %collective-permute-start.32 = (bf16[128,2048]{0,1:T(8,128)(2,1)S(1)}, bf16[128,2048]{0,1:T(8,128)(2,1)S(1)}, u32[]{:S(2)}, u32[]{:S(2)}) collective-permute-start(bf16[128,2048]{0,1:T(8,128)(2,1)S(1)} %collective-permute-done.31), channel_id=1, source_target_pairs={{0,4},{4,0},{1,5},{5,1},{2,6},{6,2},{3,7},{7,3},{8,12},{12,8},{9,1... | collective-permute-start | bytes 1572872 | tf_op jit(solution)/shard_map/ppermute | solution.py:35
  648.0 255.3 %collective-permute-start.25 = (bf16[128,2048]{0,1:T(8,128)(2,1)}, bf16[128,2048]{0,1:T(8,128)(2,1)}, u32[]{:S(2)}, u32[]{:S(2)}) collective-permute-start(bf16[128,2048]{0,1:T(8,128)(2,1)} %rev.38), channel_id=1, source_target_pairs={{0,1},{1,0},{2,3},{3,2},{4,5},{5,4},{6,7},{7,6},{8,9},{9,8},{10,11... | collective-permute-start | bytes 1572872 | tf_op jit(solution)/shard_map/ppermute | solution.py:35
  903.4 26.2 %collective-permute-start.36 = (bf16[128,2048]{0,1:T(8,128)(2,1)}, bf16[128,2048]{0,1:T(8,128)(2,1)}, u32[]{:S(2)}, u32[]{:S(2)}) collective-permute-start(bf16[128,2048]{0,1:T(8,128)(2,1)} %collective-permute-done.35), channel_id=1, source_target_pairs={{0,2},{2,0},{1,3},{3,1},{4,6},{6,4},{5,7},{7,5},{8,10},{10,8},{9,1... | collective-permute-start | bytes 1572872 | tf_op jit(solution)/shard_map/ppermute | solution.py:35
  917.2 36.4 %collective-permute-start.27 = (bf16[128,2048]{0,1:T(8,128)(2,1)}, bf16[128,2048]{0,1:T(8,128)(2,1)}, u32[]{:S(2)}, u32[]{:S(2)}) collective-permute-start(bf16[128,2048]{0,1:T(8,128)(2,1)} %collective-permute-done.26), channel_id=1, source_target_pairs={{0,4},{4,0},{1,5},{5,1},{2,6},{6,2},{3,7},{7,3},{8,12},{12,8},{9,1... | collective-permute-start | bytes 1572872 | tf_op jit(solution)/shard_map/ppermute | solution.py:35
  929.6 35.1 %collective-permute-start.37 = (bf16[128,2048]{0,1:T(8,128)(2,1)}, bf16[128,2048]{0,1:T(8,128)(2,1)}, u32[]{:S(2)}, u32[]{:S(2)}) collective-permute-start(bf16[128,2048]{0,1:T(8,128)(2,1)} %collective-permute-done.36), channel_id=1, source_target_pairs={{0,4},{4,0},{1,5},{5,1},{2,6},{6,2},{3,7},{7,3},{8,12},{12,8},{9,1... | collective-permute-start | bytes 1572872 | tf_op jit(solution)/shard_map/ppermute | solution.py:35
  936.6 30.2 %collective-permute-start.45 = (f32[128,128]{1,0:T(8,128)S(1)}, f32[128,128]{1,0:T(8,128)S(1)}, u32[]{:S(2)}, u32[]{:S(2)}) collective-permute-start(f32[128,128]{1,0:T(8,128)S(1)} %rev.42), channel_id=1, source_target_pairs={{0,1},{1,0},{2,3},{3,2},{4,5},{5,4},{6,7},{7,6},{8,9},{9,8},{10,11... | collective-permute-start | bytes 196616 | tf_op jit(solution)/shard_map/ppermute | solution.py:35
  936.7 30.1 %collective-permute-start.51 = (f32[32,128]{0,1:T(8,128)}, f32[32,128]{0,1:T(8,128)S(1)}, u32[]{:S(2)}, u32[]{:S(2)}) collective-permute-start(f32[32,128]{0,1:T(8,128)} %collective-permute-done.50), channel_id=1, source_target_pairs={{0,2},{2,0},{1,3},{3,1},{4,6},{6,4},{5,7},{7,5},{8,10},{10,8},{9,1... | collective-permute-start | bytes 49160 | tf_op jit(solution)/shard_map/ppermute | solution.py:35
  953.5 110.4 %collective-permute-start.28 = (bf16[128,2048]{0,1:T(8,128)(2,1)}, bf16[128,2048]{0,1:T(8,128)(2,1)}, u32[]{:S(2)}, u32[]{:S(2)}) collective-permute-start(bf16[128,2048]{0,1:T(8,128)(2,1)} %collective-permute-done.27), channel_id=1, source_target_pairs={{0,8},{8,0},{1,9},{9,1},{2,10},{10,2},{3,11},{11,3},{4,12},{12,4},... | collective-permute-start | bytes 1572872 | tf_op jit(solution)/shard_map/ppermute | solution.py:35
  964.8 99.8 %collective-permute-start.38 = (bf16[128,2048]{0,1:T(8,128)(2,1)}, bf16[128,2048]{0,1:T(8,128)(2,1)}, u32[]{:S(2)}, u32[]{:S(2)}) collective-permute-start(bf16[128,2048]{0,1:T(8,128)(2,1)} %collective-permute-done.37), channel_id=1, source_target_pairs={{0,8},{8,0},{1,9},{9,1},{2,10},{10,2},{3,11},{11,3},{4,12},{12,4},... | collective-permute-start | bytes 1572872 | tf_op jit(solution)/shard_map/ppermute | solution.py:35
  978.3 88.6 %collective-permute-start.54 = (f32[32,128]{0,1:T(8,128)S(1)}, f32[32,128]{0,1:T(8,128)S(1)}, u32[]{:S(2)}, u32[]{:S(2)}) collective-permute-start(f32[32,128]{0,1:T(8,128)S(1)} %collective-permute-done.53), channel_id=1, source_target_pairs={{0,16},{16,0},{1,17},{17,1},{2,18},{18,2},{3,19},{19,3},{4,20},{20... | collective-permute-start | bytes 49160 | tf_op jit(solution)/shard_map/ppermute | solution.py:35
  978.3 83.0 %collective-permute-start.42 = (f32[128,128]{1,0:T(8,128)S(1)}, f32[128,128]{1,0:T(8,128)S(1)}, u32[]{:S(2)}, u32[]{:S(2)}) collective-permute-start(f32[128,128]{1,0:T(8,128)S(1)} %collective-permute-done.41), channel_id=1, source_target_pairs={{0,4},{4,0},{1,5},{5,1},{2,6},{6,2},{3,7},{7,3},{8,12},{12,8},{9,1... | collective-permute-start | bytes 196616 | tf_op jit(solution)/shard_map/ppermute | solution.py:35
  978.4 83.2 %collective-permute-start.48 = (f32[128,128]{1,0:T(8,128)S(1)}, f32[128,128]{1,0:T(8,128)}, u32[]{:S(2)}, u32[]{:S(2)}) collective-permute-start(f32[128,128]{1,0:T(8,128)S(1)} %collective-permute-done.47), channel_id=1, source_target_pairs={{0,8},{8,0},{1,9},{9,1},{2,10},{10,2},{3,11},{11,3},{4,12},{12,4},... | collective-permute-start | bytes 196616 | tf_op jit(solution)/shard_map/ppermute | solution.py:35
  1064.0 27.2 %collective-permute-start.29 = (bf16[128,2048]{0,1:T(8,128)(2,1)}, bf16[128,2048]{0,1:T(8,128)(2,1)S(1)}, u32[]{:S(2)}, u32[]{:S(2)}) collective-permute-start(bf16[128,2048]{0,1:T(8,128)(2,1)} %collective-permute-done.28), channel_id=1, source_target_pairs={{0,16},{16,0},{1,17},{17,1},{2,18},{18,2},{3,19},{19,3},{4,20},{20... | collective-permute-start | bytes 1572872 | tf_op jit(solution)/shard_map/ppermute | solution.py:35
  1064.5 26.7 %collective-permute-start.39 = (bf16[128,2048]{0,1:T(8,128)(2,1)}, bf16[128,2048]{0,1:T(8,128)(2,1)S(1)}, u32[]{:S(2)}, u32[]{:S(2)}) collective-permute-start(bf16[128,2048]{0,1:T(8,128)(2,1)} %collective-permute-done.38), channel_id=1, source_target_pairs={{0,16},{16,0},{1,17},{17,1},{2,18},{18,2},{3,19},{19,3},{4,20},{20... | collective-permute-start | bytes 1572872 | tf_op jit(solution)/shard_map/ppermute | solution.py:35
  (114 other events, 2606.8 us)
Sparse Core Ops, SparseCore 0:
  16.7 231.6 all-gather.14
  250.3 197.4 all-gather.10
  449.7 184.5 all-gather.12
  635.9 184.8 all-gather.16
where the time goes:
time: 1120 us; the launch traced here: 1100 us
  waiting for transfers between devices  577 us (52%)
  blocking collectives  171 us (15%)
  other arithmetic  127 us (11%)
  local copies, waits for them, and re-layouts  89.2 us (8%)
  matrix products  60.9 us (5%)
  starting transfers between devices  60 us (5%)
  between operations  15.9 us (1%)
    all_gather x4, waiting for transfers between devices, entering_2(): gathered = jax.tree.map(lambda a: lax.all_gather(a, axis), part)  310 us
    ppermute x55, waiting for transfers between devices, partner(): return lax.ppermute(block, axis, route)  268 us
    add x62, other arithmetic, scan_join(): later[0][:, None, None] * earlier[1] + later[1]  89.8 us
    all_gather x2, blocking collectives, entering_2(): gathered = jax.tree.map(lambda a: lax.all_gather(a, axis), part)  89.4 us
    psum x1, blocking collectives, body(): lax.psum((jnp.stack([fwd[5], rev[5]]), jnp.stack([fwd[6], rev[6]]), skip_...  81.9 us
    ppermute x55, starting transfers between devices, partner(): return lax.ppermute(block, axis, route)  59.8 us
    mul x62, local copies, waits for them, and re-layouts, scan_join(): later[0][:, None, None] * earlier[1] + later[1]  42.7 us
    dot_general x6, matrix products, group_outputs(): inside = jnp.einsum('khqs,kshp->kqhp', mixing, driven, precision=highest)  30.8 us
  transfers between devices with their start and end apart: 59, of which 32 were waited for; matrix products, arithmetic and copies ran while one was open for 24% of the time, Pallas kernels for 0%

commit v1 on v0

v1 whole, which is shorter than its diff:
```python
import functools

import jax
import jax.numpy as jnp
from jax import lax
from jax.experimental import pallas as pl
from jax.experimental.pallas import tpu as pltpu
from jax.sharding import PartitionSpec as P

F32 = jnp.float32
BF16 = jnp.bfloat16
MESH = pl.DeviceIdType.MESH
TOK = 128
LANES = 128
HIGH = lax.Precision.HIGHEST

SCAN_DIR = (0, 1, 1, 0)
SCAN_LEFT = (False, False, True, True)


def dot(a, b, dims=((1,), (0,)), precision=None):
    return lax.dot_general(
        a, b, (dims, ((), ())), precision=precision, preferred_element_type=F32
    )


def iota(shape, axis):
    return lax.broadcasted_iota(jnp.int32, shape, axis)


def split2(v):
    hi = v.astype(BF16)
    return hi, (v - hi.astype(F32)).astype(BF16)


def split3(v):
    hi = v.astype(BF16)
    rest = v - hi.astype(F32)
    mid = rest.astype(BF16)
    return hi, mid, (rest - mid.astype(F32)).astype(BF16)


def column(row):
    heads = row.shape[1]
    eye = iota((heads, heads), 0) == iota((heads, heads), 1)
    return jnp.sum(jnp.where(eye, jnp.broadcast_to(row, (heads, heads)), 0.0), axis=1, keepdims=True)


def softplus(v):
    z = jnp.exp(-jnp.abs(v))
    u = z / (2.0 + z)
    q = u * u
    series = 1.0 / 17.0
    for term in (15.0, 13.0, 11.0, 9.0, 7.0, 5.0, 3.0, 1.0):
        series = series * q + 1.0 / term
    return jnp.maximum(v, 0.0) + 2.0 * u * series


def timing(raw, log_decay, step_bias, mask, r):
    rate = -jnp.exp(column(log_decay[r : r + 1, :]))
    shifted = raw + column(step_bias[r : r + 1, :])
    soft = softplus(shifted)
    slope = 1.0 / (1.0 + jnp.exp(-shifted))
    steps = soft * mask
    logs = steps * rate
    upto = (iota((TOK, TOK), 0) <= iota((TOK, TOK), 1)).astype(F32)
    cum = dot(logs, upto, precision=HIGH)
    total = cum[:, TOK - 1 :]
    if r == 0:
        place = cum
        weight = jnp.exp(total - cum) * steps
        decay = jnp.exp(cum)
    else:
        place = cum - logs
        weight = jnp.exp(place) * steps
        decay = jnp.exp(total - place)
    return dict(
        rate=rate, soft=soft, slope=slope, steps=steps, total=total, place=place,
        weight=weight, decay=decay,
    )


def spread(pair, tile):
    rows = pair.shape[0]
    heads = rows // 2
    pick = iota((rows, LANES), 0)
    pick = jnp.where(pick >= heads, pick - heads, pick)
    mine = 2 * tile + (iota((rows, LANES), 1) >= LANES // 2).astype(jnp.int32)
    sel = jnp.where(pick == mine, 1.0, 0.0).astype(BF16)
    return dot(pair, sel, ((0,), (0,)))


def two_parts(v):
    hi, lo = split2(v)
    return jnp.concatenate([hi.astype(F32), lo.astype(F32)], axis=0).astype(BF16)


UNROLL = 2
PLAN = (5, 4, 4, 2, 1)
LINK = (BF16, BF16, BF16, F32, F32)


def pair_rows(v):
    hi, lo = split2(v)
    return jnp.concatenate([hi, lo], axis=0)


def pair_lanes(v):
    hi, lo = split2(v)
    return jnp.concatenate([hi, lo], axis=1)


def layer_kernel(
    x_ref, g_ref, key_ref, query_ref, raw_ref, ld_ref, sb_ref, skip_ref, valid_ref,
    out_ref, pg_ref, kg_ref, qg_ref, sg_ref, dec_ref, bias_ref, skipg_ref,
    seg, seg_in, coef, own, got, snd, eown, egot, esnd, e_hi, e_lo,
    y_ref, dx_ref, ge_ref, ds_ref, dk_ref, dq_ref, sums_ref, part_a, part_b, part_c,
    up_send, up_recv, down_send, down_recv, log_send, log_recv,
    sum_send, sum_recv, *, levels, units, tiles, line, rows_of, groups
):
    me = lax.axis_index("seq")
    my_dp = lax.axis_index("dp")
    bits = [(me // (1 << b)) % 2 for b in range(levels)]
    peers = [me + (1 << b) * (1 - 2 * bits[b]) for b in range(levels)]
    half = [units >> (b + 1) for b in range(levels)]
    base = [0]
    for b in range(levels):
        base.append(base[b] + bits[b] * half[b])

    in_line = me % line
    my_line = me // line
    sum_peers = (
        [{"seq": my_line * line + (in_line + k) % line} for k in range(1, line)],
        [{"seq": (my_line + k) % rows_of * line + in_line} for k in range(1, rows_of)],
        [{"dp": (my_dp + k) % groups} for k in range(1, groups)],
    )
    sum_place = (in_line, my_line, my_dp)
    sum_size = (line, rows_of, groups)

    barrier = pltpu.get_barrier_semaphore()
    greeted = 0
    for group in sum_peers:
        for device in group:
            pl.semaphore_signal(barrier, inc=1, device_id=device, device_id_type=MESH)
            greeted += 1

    mask = valid_ref[0, 0].astype(F32)
    raw = raw_ref[...]
    logd = ld_ref[...]
    bias = sb_ref[...]
    heads = raw.shape[0]
    t = [timing(raw, logd, bias, mask, r) for r in (0, 1)]
    pick = iota((tiles, heads), 1)
    even = (pick == 2 * iota((tiles, heads), 0)).astype(F32)
    odd = (pick == 2 * iota((tiles, heads), 0) + 1).astype(F32)
    left_row = iota((tiles, LANES), 1) < LANES // 2
    for r in (0, 1):
        wide = jnp.broadcast_to(t[r]["total"], (heads, LANES))
        seg[0, r] = jnp.where(
            left_row, dot(even, wide, precision=HIGH), dot(odd, wide, precision=HIGH)
        )
    w = [two_parts(t[r]["weight"]) for r in (0, 1)]
    e = [two_parts(t[r]["decay"]) for r in (0, 1)]
    key = key_ref[...]
    query = query_ref[...]

    pl.semaphore_wait(barrier, greeted)

    def push(src, dst, send, recv, b):
        return pltpu.make_async_remote_copy(
            src_ref=src, dst_ref=dst, send_sem=send, recv_sem=recv,
            device_id={"seq": peers[b]}, device_id_type=MESH,
        )

    def up_copy(b, a):
        return push(snd[b].at[a], got[b].at[a], up_send.at[b, a], up_recv.at[b, a], b)

    def down_copy(b, a):
        if b == 0:
            dst = e_hi.at[a, pl.ds(bits[0] * half[0], half[0])]
        else:
            dst = egot[b].at[a]
        return push(esnd[b].at[a], dst, down_send.at[b, a], down_recv.at[b, a], b)

    def log_copy(b):
        return push(seg.at[b], seg_in.at[b], log_send.at[b], log_recv.at[b], b)

    def late_flag(b, a):
        late = (1 - bits[b]) if SCAN_LEFT[a] else bits[b]
        return late.astype(F32)

    def factors(b):
        log_copy(b).wait_recv()
        mine, other = seg[b], seg_in[b]
        if b + 1 < levels:
            seg[b + 1] = mine + other
            log_copy(b + 1).start()
        for a in range(4):
            r = SCAN_DIR[a]
            late = late_flag(b, a)
            coef[b, a, 0] = jnp.exp((1.0 - late) * other[r])
            coef[b, a, 1] = jnp.exp(late * mine[r])
            coef[b, a, 2] = jnp.exp(late * other[r])
            coef[b, a, 3] = jnp.exp((1.0 - late) * mine[r])

    log_copy(0).start()

    key_t = key.astype(F32).T.astype(BF16)
    query_t = query.astype(F32).T.astype(BF16)
    key_tt = jnp.concatenate([key_t, key_t], axis=1)
    query_tt = jnp.concatenate([query_t, query_t], axis=1)
    half_tiles = tiles // 2
    scale = (w[0], e[1], w[1], e[0])
    for a in range(4):
        is_state = a % 2 == 0
        ref, lhs = (x_ref, key_tt) if is_state else (g_ref, query_tt)

        def state(j, ref=ref, lhs=lhs, a=a, is_state=is_state):
            lanes = pl.ds(pl.multiple_of(j * LANES, LANES), LANES)
            v = ref[:, lanes].astype(F32) * spread(scale[a], j)
            if not is_state:
                v = v * mask
            return dot(lhs, pair_rows(v)).reshape(2, TOK // 2, LANES)

        def state_out(i, carry, a=a, state=state):
            u = state((1 - bits[0]) * half_tiles + i)
            snd[0][a, pl.ds(2 * i, 2)] = u.astype(snd[0].dtype)
            return carry

        def state_keep(i, carry, a=a, state=state):
            own[0][a, pl.ds(2 * i, 2)] = state(bits[0] * half_tiles + i)
            return carry

        lax.fori_loop(0, half_tiles, state_out, 0, unroll=UNROLL)
        up_copy(0, a).start()
        lax.fori_loop(0, half_tiles, state_keep, 0, unroll=UNROLL)
        if a < levels:
            factors(a)
    for b in range(4, levels):
        factors(b)

    scores = dot(query, key, ((1,), (1,)))
    scores_t = dot(key, query, ((1,), (1,)))
    sign = (1.0, -1.0)
    at = [sign[r] * t[r]["place"] for r in (0, 1)]
    frm = [sign[r] * t[r]["place"] - jnp.log(t[r]["soft"]) for r in (0, 1)]

    def three(v):
        parts = [p.astype(F32) for p in split3(v)]
        return jnp.concatenate(parts, axis=0).T.astype(BF16)

    at_cols = [three(v) for v in at]
    frm_cols = [three(v) for v in frm]
    rows_i, cols_i = iota((TOK, TOK), 0), iota((TOK, TOK), 1)
    lower, upper = rows_i >= cols_i, rows_i <= cols_i
    left = iota((TOK, LANES), 1) < LANES // 2
    ds_ref[...] = jnp.zeros_like(ds_ref)
    dk_ref[...] = jnp.zeros_like(dk_ref)
    dq_ref[...] = jnp.zeros_like(dq_ref)
    sums_ref[...] = jnp.zeros_like(sums_ref)
    head_row = iota((heads, TOK), 0)

    def row_of(v, h):
        return jnp.sum(jnp.where(head_row == h, v, 0.0), axis=0, keepdims=True)

    def inside(j, carry):
        lanes = pl.ds(pl.multiple_of(j * LANES, LANES), LANES)
        xb = x_ref[:, lanes]
        x = xb.astype(F32)
        g = g_ref[:, lanes].astype(F32) * mask
        zero = jnp.zeros_like(x)
        x_0, x_1 = jnp.where(left, x, zero).astype(BF16), jnp.where(left, zero, x).astype(BF16)
        g_0, g_1 = jnp.where(left, g, zero).astype(BF16), jnp.where(left, zero, g).astype(BF16)
        x_cat = jnp.concatenate([x_0, x_0, x_1, x_1], axis=0)
        g_cat = jnp.concatenate([g_0, g_0, g_1, g_1], axis=0)
        d_m = dot(jnp.concatenate([g_0, g_1], axis=0), xb, ((1,), (1,)))
        pick = iota((3 * heads, 2 * LANES), 0) % heads
        mine = 2 * j + (iota((3 * heads, 2 * LANES), 1) >= LANES).astype(jnp.int32)
        sel = jnp.where(pick == mine, 1.0, 0.0).astype(BF16)
        wsum = [0.0, 0.0]
        for r in (0, 1):
            at_b = dot(at_cols[r], sel)
            frm_b = dot(frm_cols[r], sel)
            m, m_t = [], []
            for k in (0, 1):
                at_row = row_of(at[r], 2 * j + k)
                frm_row = row_of(frm[r], 2 * j + k)
                cut = slice(k * LANES, (k + 1) * LANES)
                keep, keep_t = (lower, upper) if r == 0 else (upper, lower)
                wide = jnp.exp(jnp.where(keep, at_b[:, cut] - frm_row, -1e30))
                wide_t = jnp.exp(jnp.where(keep_t, at_row - frm_b[:, cut], -1e30))
                wsum[k] = wsum[k] + wide
                m += split2(wide * scores)
                m_t += split2(wide_t * scores_t)
            y_ref[r, j] = dot(jnp.concatenate(m, axis=1), x_cat)
            dx_ref[r, j] = dot(jnp.concatenate(m_t, axis=1), g_cat)
        ds_ref[...] += d_m[:TOK] * wsum[0] + d_m[TOK:] * wsum[1]
        return carry

    done = [0]

    def inside_some(count):
        stop = min(done[0] + count, tiles)
        if stop > done[0]:
            lax.fori_loop(done[0], stop, inside, 0)
        done[0] = stop

    def row(b, a, which, unit):
        return coef[b, a, which, pl.ds(unit // 2, 1), :]

    def joined(b, a, i):
        unit = base[b + 1] + i
        return row(b, a, 0, unit) * own[b][a, i] + row(b, a, 1, unit) * got[b][a, i].astype(F32)

    inside_some(PLAN[0])
    for b in range(1, levels):
        for a in range(4):
            up_copy(b - 1, a).wait_recv()

            def to_send(i, carry, b=b, a=a):
                snd[b][a, i] = joined(b - 1, a, (1 - bits[b]) * half[b] + i).astype(snd[b].dtype)
                return carry

            def to_keep(i, carry, b=b, a=a):
                own[b][a, i] = joined(b - 1, a, bits[b] * half[b] + i)
                return carry

            lax.fori_loop(0, half[b], to_send, 0, unroll=min(UNROLL, half[b]))
            up_copy(b, a).start()
            lax.fori_loop(0, half[b], to_keep, 0, unroll=min(UNROLL, half[b]))
        inside_some(PLAN[b])

    for b in range(levels - 1, -1, -1):
        if b == 0:
            inside_some(tiles)
        for a in range(4):
            late = late_flag(b, a)
            if b == levels - 1:
                up_copy(b, a).wait_recv()
            else:
                down_copy(b + 1, a).wait_recv()

            def entering(i, where, b=b, a=a):
                if where == "own":
                    return eown[b + 1][a, i]
                return egot[b + 1][a, i].astype(F32)

            def for_peer(i, at_unit, where, b=b, a=a, late=late):
                value = (1.0 - late) * own[b][a, at_unit]
                if where is not None:
                    value += row(b, a, 3, base[b + 1] + at_unit) * entering(i, where)
                esnd[b][a, at_unit] = value.astype(esnd[b].dtype)

            def for_me(i, at_unit, where, b=b, a=a, late=late):
                value = late * got[b][a, at_unit].astype(F32)
                if where is not None:
                    value += row(b, a, 2, base[b + 1] + at_unit) * entering(i, where)
                if b == 0:
                    hi, lo = split2(value)
                    e_hi[a, bits[0] * half[0] + at_unit] = hi
                    e_lo[a, bits[0] * half[0] + at_unit] = lo
                    e_lo[a, (1 - bits[0]) * half[0] + at_unit] = jnp.zeros_like(lo)
                else:
                    eown[b][a, at_unit] = value

            def sweep(fn, b=b):
                if b == levels - 1:
                    lax.fori_loop(0, half[b], lambda i, c: (fn(i, i, None), c)[1], 0)
                    return
                h = half[b + 1]
                n = min(UNROLL, h)
                mine, other = bits[b + 1] * h, (1 - bits[b + 1]) * h
                lax.fori_loop(0, h, lambda i, c: (fn(i, mine + i, "own"), c)[1], 0, unroll=n)
                lax.fori_loop(0, h, lambda i, c: (fn(i, other + i, "got"), c)[1], 0, unroll=n)

            sweep(for_peer)
            down_copy(b, a).start()
            sweep(for_me)

    skip2 = two_parts(jnp.broadcast_to(column(skip_ref[...]), (heads, TOK)))
    query2 = jnp.concatenate([query, query], axis=1)
    key2 = jnp.concatenate([key, key], axis=1)

    def carried(j):
        lanes = pl.ds(pl.multiple_of(j * LANES, LANES), LANES)
        x = x_ref[:, lanes].astype(F32)
        g = g_ref[:, lanes].astype(F32) * mask
        tile = pl.ds(2 * j, 2)

        def parts(a):
            hi = e_hi[a, tile].reshape(TOK, LANES)
            lo = e_lo[a, tile].reshape(TOK, LANES)
            return jnp.concatenate([hi, lo], axis=0), jnp.concatenate([hi, hi], axis=1), hi, lo

        enter = (parts(0), parts(2))
        back = (parts(3), parts(1))
        quant, y, dx = [], [], []
        for r in (0, 1):
            w_b, e_b = spread(w[r], j), spread(e[r], j)
            yr = y_ref[r, j] + e_b * dot(query2, enter[r][0])
            col_carried = w_b * dot(key2, back[r][0])
            dxr = dx_ref[r, j] + col_carried
            quant += [g * yr, x * dxr, x * col_carried]
            dk_ref[...] += dot(pair_lanes(x * w_b), back[r][1], ((1,), (1,)))
            dq_ref[...] += dot(pair_lanes(g * e_b), enter[r][1], ((1,), (1,)))
            through = (enter[r][2].astype(F32) + enter[r][3].astype(F32)) * (
                back[r][2].astype(F32) + back[r][3].astype(F32)
            )
            ge_ref[r, :, lanes] = jnp.sum(through.reshape(TOK // 8, 8, LANES), axis=0)
            y.append(yr)
            dx.append(dxr)
        quant.append(g * x)
        head_lane = 2 * j + (iota((heads, LANES), 1) >= LANES // 2).astype(jnp.int32)
        ones = jnp.where(iota((heads, LANES), 0) == head_lane, 1.0, 0.0).astype(BF16)
        ones2 = jnp.concatenate([ones, ones], axis=1)
        for n, q in enumerate(quant):
            sums_ref[n] += dot(ones2, pair_lanes(q), ((1,), (1,)))
        skip_b = spread(skip2, j)
        out_ref[:, lanes] = (mask * (y[0] + y[1] + skip_b * x)).astype(BF16)
        pg_ref[:, lanes] = (dx[0] + dx[1] + skip_b * g).astype(BF16)

    lax.fori_loop(0, half_tiles, lambda i, c: (carried(bits[0] * half_tiles + i), c)[1], 0)
    for a in range(4):
        down_copy(0, a).wait_recv()
    lax.fori_loop(0, half_tiles, lambda i, c: (carried((1 - bits[0]) * half_tiles + i), c)[1], 0)

    ds_hi, ds_lo = split2(ds_ref[...])
    qg_ref[...] = dq_ref[...] + dot(jnp.concatenate([ds_hi, ds_lo], axis=1), jnp.concatenate([key, key], axis=0))
    kg_ref[...] = (
        dk_ref[...] + dot(ds_hi, query, ((0,), (0,))) + dot(ds_lo, query, ((0,), (0,)))
    )

    width = tiles * LANES
    all_ones = jnp.where(
        iota((heads, width), 0) == iota((heads, width), 1) // (LANES // 2), 1.0, 0.0
    ).astype(BF16)
    upto = (rows_i <= cols_i).astype(F32)
    since = (rows_i >= cols_i).astype(F32)
    ones_row = jnp.ones((8, TOK), F32)

    def total_row(v):
        return dot(ones_row, v, ((1,), (1,)), precision=HIGH)[0:1]

    step_grad = jnp.zeros((heads, TOK), F32)
    decay_rows, bias_rows = [], []
    for r in (0, 1):
        hi, lo = split2(ge_ref[r])
        passing = jnp.sum(
            dot(all_ones, hi, ((1,), (1,))) + dot(all_ones, lo, ((1,), (1,))),
            axis=1, keepdims=True,
        )
        row_dot, col_dot, flow = sums_ref[3 * r], sums_ref[3 * r + 1], sums_ref[3 * r + 2]
        flow = jnp.exp(t[r]["total"]) * passing + jnp.sum(flow, axis=1, keepdims=True)
        d_log = flow + dot(row_dot - col_dot, since if r == 0 else upto, precision=HIGH)
        slope = t[r]["slope"] * mask
        raw_grad = col_dot * (slope / t[r]["soft"]) + t[r]["rate"] * d_log * slope
        step_grad += raw_grad
        decay_rows.append(-jnp.exp(logd[r : r + 1, :]) * total_row(t[r]["steps"] * d_log))
        bias_rows.append(total_row(raw_grad))
    sg_ref[...] = step_grad

    skip_row = total_row(sums_ref[6])
    value = jnp.concatenate(
        [
            jnp.concatenate(decay_rows + bias_rows, axis=1),
            jnp.concatenate([skip_row] * 4, axis=1),
        ],
        axis=0,
    )
    for n, part in enumerate((part_a, part_b, part_c)):
        place, size = sum_place[n], sum_size[n]
        part[place] = value
        for k in range(1, size):
            pltpu.make_async_remote_copy(
                src_ref=part.at[place], dst_ref=part.at[place],
                send_sem=sum_send.at[n, k], recv_sem=sum_recv.at[n, place],
                device_id=sum_peers[n][k - 1], device_id_type=MESH,
            ).start()
        for k in range(1, size):
            other = (place + k) % size
            pltpu.make_async_remote_copy(
                src_ref=part.at[other], dst_ref=part.at[other],
                send_sem=sum_send.at[n, k], recv_sem=sum_recv.at[n, other],
                device_id=sum_peers[n][k - 1], device_id_type=MESH,
            ).wait_recv()
        value = part[0]
        for k in range(1, size):
            value += part[k]
    for r in (0, 1):
        dec_ref[r : r + 1, :] = value[0:1, r * heads : (r + 1) * heads]
        bias_ref[r : r + 1, :] = value[0:1, (2 + r) * heads : (3 + r) * heads]
    skipg_ref[...] = value[1:2, :heads]

    for b in range(levels):
        log_copy(b).wait_send()
        for a in range(4):
            up_copy(b, a).wait_send()
            down_copy(b, a).wait_send()
    for n, part in enumerate((part_a, part_b, part_c)):
        for k in range(1, sum_size[n]):
            pltpu.make_async_remote_copy(
                src_ref=part.at[sum_place[n]], dst_ref=part.at[sum_place[n]],
                send_sem=sum_send.at[n, k], recv_sem=sum_recv.at[n, sum_place[n]],
                device_id=sum_peers[n][k - 1], device_id_type=MESH,
            ).wait_send()


def body(
    patches, key_proj, query_proj, step_raw, log_decay, step_bias, skip_gain, group_valid, out_grad
):
    heads = step_raw.shape[1]
    width = patches.shape[2]
    tiles = width // LANES
    units = 2 * tiles
    seq = lax.axis_size("seq")
    groups = lax.axis_size("dp")
    levels = seq.bit_length() - 1
    line = min(8, seq)
    rows_of = seq // line
    vmem = pl.BlockSpec(memory_space=pltpu.VMEM)
    h = [units >> (b + 1) for b in range(levels)]
    unit = (TOK // 2, LANES)
    link = [LINK[b] for b in range(levels)]

    def blocks(dtypes):
        return [pltpu.VMEM((4, h[b]) + unit, dtypes[b]) for b in range(levels)]

    wide = [F32] * levels
    dma = pltpu.SemaphoreType.DMA
    size = max(line, rows_of, groups)
    output, patch_grad, key_grad, query_grad, step_grad, decay_grad, bias_grad, skip_grad = (
        pl.pallas_call(
            functools.partial(
                layer_kernel, levels=levels, units=units, tiles=tiles,
                line=line, rows_of=rows_of, groups=groups,
            ),
            out_shape=(
                jax.ShapeDtypeStruct((TOK, width), BF16),
                jax.ShapeDtypeStruct((TOK, width), BF16),
                jax.ShapeDtypeStruct((TOK, LANES), F32),
                jax.ShapeDtypeStruct((TOK, LANES), F32),
                jax.ShapeDtypeStruct((heads, TOK), F32),
                jax.ShapeDtypeStruct((2, heads), F32),
                jax.ShapeDtypeStruct((2, heads), F32),
                jax.ShapeDtypeStruct((1, heads), F32),
            ),
            in_specs=[vmem] * 8 + [pl.BlockSpec(memory_space=pltpu.SMEM)],
            out_specs=(vmem,) * 8,
            scratch_shapes=[
                pltpu.VMEM((levels, 2, tiles, LANES), F32),
                pltpu.VMEM((levels, 2, tiles, LANES), F32),
                pltpu.VMEM((levels, 4, 4, tiles, LANES), F32),
                blocks(wide),
                blocks(link),
                blocks(link),
                blocks(wide),
                blocks(link),
                blocks(link),
                pltpu.VMEM((4, units) + unit, BF16),
                pltpu.VMEM((4, units) + unit, BF16),
                pltpu.VMEM((2, tiles, TOK, LANES), F32),
                pltpu.VMEM((2, tiles, TOK, LANES), F32),
                pltpu.VMEM((2, 8, width), F32),
                pltpu.VMEM((TOK, TOK), F32),
                pltpu.VMEM((TOK, LANES), F32),
                pltpu.VMEM((TOK, LANES), F32),
                pltpu.VMEM((7, heads, TOK), F32),
                pltpu.VMEM((line, 2, LANES), F32),
                pltpu.VMEM((rows_of, 2, LANES), F32),
                pltpu.VMEM((groups, 2, LANES), F32),
                dma((levels, 4)),
                dma((levels, 4)),
                dma((levels, 4)),
                dma((levels, 4)),
                dma((levels,)),
                dma((levels,)),
                dma((3, size)),
                dma((3, size)),
            ],
            compiler_params=pltpu.CompilerParams(collective_id=0, has_side_effects=True),
            name="layer",
        )(
            patches[0], out_grad[0], key_proj[0], query_proj[0], step_raw[0],
            log_decay, step_bias, skip_gain[None], group_valid,
        )
    )
    return (
        output[None],
        patch_grad[None],
        key_grad[None],
        query_grad[None],
        step_grad[None],
        decay_grad,
        bias_grad,
        skip_grad[0],
    )


def solution(mesh):
    in_specs = (
        P("dp", "seq", None),
        P("dp", "seq", None),
        P("dp", "seq", None),
        P("dp", None, "seq"),
        P(),
        P(),
        P(),
        P("dp", "seq"),
        P("dp", "seq", None),
    )
    out_specs = (
        P("dp", "seq", None),
        P("dp", "seq", None),
        P("dp", "seq", None),
        P("dp", "seq", None),
        P("dp", None, "seq"),
        P(),
        P(),
        P(),
    )
    return jax.shard_map(body, mesh=mesh, in_specs=in_specs, out_specs=out_specs, check_vma=False)
```

time: 1120 us -> 112 us (0.10); the launches traced: 1100 us -> 112 us
  waiting for transfers between devices: 577 us -> 0 us
  blocking collectives: 171 us -> 0 us
  other arithmetic: 127 us -> 0 us
  Pallas kernels: 0 us -> 103 us
  local copies, waits for them, and re-layouts: 89.2 us -> 6.8 us
  matrix products: 60.9 us -> 0 us
  starting transfers between devices: 60 us -> 0 us
  between operations: 15.9 us -> 1.31 us
    all_gather x4 -> x0, waiting for transfers between devices: 310 us -> none  [entering_2(): gathered = jax.tree.map(lambda a: lax.all_gather(a, axis), part)]
    ppermute x55 -> x0, waiting for transfers between devices: 268 us -> none  [partner(): return lax.ppermute(block, axis, route)]
    pallas_call x0 -> x1, Pallas kernels: none -> 103 us  [body(): pl.pallas_call(functools.partial(layer_kernel, levels=levels, units=units...]
    add x65 -> x0, other arithmetic: 90.6 us -> none  [the longest x62 89.8 us: scan_join(): later[0][:, None, None] * earlier[1] + later[1]]
    all_gather x2 -> x0, blocking collectives: 89.4 us -> none  [entering_2(): gathered = jax.tree.map(lambda a: lax.all_gather(a, axis), part)]
    psum x1 -> x0, blocking collectives: 81.9 us -> none  [body(): lax.psum((jnp.stack([fwd[5], rev[5]]), jnp.stack([fwd[6], rev[6]]), skip_...]
    dot_general x24 -> x0, matrix products: 60.9 us -> none  [the longest x6 30.8 us: group_outputs(): inside = jnp.einsum('khqs,kshp->kqhp', mixing, driven, precision=highest)]
    ppermute x55 -> x0, starting transfers between devices: 59.8 us -> none  [partner(): return lax.ppermute(block, axis, route)]
  transfers between devices with their start and end apart: 59 -> 0, of which waited for: 32 -> 0; matrix products, arithmetic and copies ran while one was open for 24% -> 0% of each run, Pallas kernels for 0% -> 0%
where the time goes in v1:
time: 112 us
  Pallas kernels  103 us (92%)
  local copies, waits for them, and re-layouts  6.8 us (6%)
  between operations  1.31 us (1%)
    pallas_call x1, Pallas kernels, body(): pl.pallas_call(functools.partial(layer_kernel, levels=levels, units=units...  103 us
    unnamed x22, local copies, waits for them, and re-layouts  6.8 us

profile of v1, /device:TPU:1, one launch (start us, length us, event | category | flops | bytes accessed | tf_op | source)
XLA Modules:
  0.0 111.6 jit_solution(966958094678758284)
XLA Ops:
  1.3 103.5 %layer.1 = (bf16[128,2048]{1,0:T(8,128)(2,1)}, bf16[128,2048]{1,0:T(8,128)(2,1)}, f32[128,128]{1,0:T(8,128)}, f32[128,128]{1,0:T(8,128)}, f32[32,128]{1,0:T(8,12...) custom-call(bf16[128,2048]{1,0:T(8,128)(2,1)} %bitcast.12, bf16[128,2048]{1,0:T(8,128)(2,1)} %bitcast.13, ...), custom_call_target="tpu_custom_call" | custom-call | tf_op jit(solution)/shard_map/layer/pallas_call | solution.py:532
  104.8 0.0 copy-start
  104.8 1.9 %copy.26 = bf16[1,128,2048]{2,1,0:T(8,128)(2,1)} copy(bf16[1,128,2048]{2,1,0:T(8,128)(2,1)} %bitcast.15) | data formatting | bytes 1048576
  106.7 0.0 copy-done
  106.7 0.0 copy-start.2
  106.7 0.8 copy.27
  107.5 0.1 copy-done.2
  107.6 0.0 copy-start.1
  107.6 0.6 copy.28
  108.2 0.2 copy-done.1
  108.4 0.0 copy-start.3
  108.5 0.6 copy.29
  109.1 0.1 copy-done.3
  109.2 0.0 copy-start.5
  109.2 0.6 copy.30
  109.8 0.0 copy-done.5
  109.8 0.0 copy-start.4
  109.8 0.6 copy.31
  110.4 0.1 copy-done.4
  110.5 0.0 copy-start.6
  110.5 0.6 copy.32
  111.0 0.0 copy-done.6
  111.1 0.5 copy.33
Async XLA Ops:
  104.8 2.0 %copy-start = (bf16[128,2048]{1,0:T(8,128)(2,1)S(1)}, bf16[128,2048]{1,0:T(8,128)(2,1)}, u32[]{:S(2)}) copy-start(bf16[128,2048]{1,0:T(8,128)(2,1)} %get-tuple-element.17) | copy-start | bytes 1572868
  106.7 0.9 copy-start.2
  107.6 0.9 copy-start.1
  108.4 0.7 copy-start.3
  109.2 0.6 copy-start.5
  109.8 0.7 copy-start.4
  110.5 0.6 copy-start.6

commit v2 on v1

v2 whole, which is shorter than its diff:
```python
import functools

import jax
import jax.numpy as jnp
from jax import lax
from jax.experimental import pallas as pl
from jax.experimental.pallas import tpu as pltpu
from jax.sharding import PartitionSpec as P

F32 = jnp.float32
BF16 = jnp.bfloat16
MESH = pl.DeviceIdType.MESH
TOK = 128
LANES = 128
HIGH = lax.Precision.HIGHEST

SCAN_DIR = (0, 1, 1, 0)
SCAN_LEFT = (False, False, True, True)


def dot(a, b, dims=((1,), (0,)), precision=None):
    return lax.dot_general(
        a, b, (dims, ((), ())), precision=precision, preferred_element_type=F32
    )


def iota(shape, axis):
    return lax.broadcasted_iota(jnp.int32, shape, axis)


def split2(v):
    hi = v.astype(BF16)
    return hi, (v - hi.astype(F32)).astype(BF16)


def split3(v):
    hi = v.astype(BF16)
    rest = v - hi.astype(F32)
    mid = rest.astype(BF16)
    return hi, mid, (rest - mid.astype(F32)).astype(BF16)


def column(row):
    heads = row.shape[1]
    eye = iota((heads, heads), 0) == iota((heads, heads), 1)
    return jnp.sum(jnp.where(eye, jnp.broadcast_to(row, (heads, heads)), 0.0), axis=1, keepdims=True)


def softplus(v):
    z = jnp.exp(-jnp.abs(v))
    u = z / (2.0 + z)
    q = u * u
    series = 1.0 / 17.0
    for term in (15.0, 13.0, 11.0, 9.0, 7.0, 5.0, 3.0, 1.0):
        series = series * q + 1.0 / term
    return jnp.maximum(v, 0.0) + 2.0 * u * series


def timing(raw, log_decay, step_bias, mask, r):
    rate = -jnp.exp(column(log_decay[r : r + 1, :]))
    shifted = raw + column(step_bias[r : r + 1, :])
    soft = softplus(shifted)
    slope = 1.0 / (1.0 + jnp.exp(-shifted))
    steps = soft * mask
    logs = steps * rate
    upto = (iota((TOK, TOK), 0) <= iota((TOK, TOK), 1)).astype(F32)
    cum = dot(logs, upto, precision=HIGH)
    total = cum[:, TOK - 1 :]
    if r == 0:
        place = cum
        weight = jnp.exp(total - cum) * steps
        decay = jnp.exp(cum)
    else:
        place = cum - logs
        weight = jnp.exp(place) * steps
        decay = jnp.exp(total - place)
    return dict(
        rate=rate, soft=soft, slope=slope, steps=steps, total=total, place=place,
        weight=weight, decay=decay,
    )


def spread(pair, tile):
    rows = pair.shape[1]
    pick = iota((rows, LANES), 0) % (rows // 2)
    mine = 2 * tile + (iota((rows, LANES), 1) >= LANES // 2).astype(jnp.int32)
    return dot(pair, jnp.where(pick == mine, 1.0, 0.0).astype(BF16))


def parts_t(parts):
    return jnp.concatenate([p.astype(F32) for p in parts], axis=0).T.astype(BF16)


ARRAYS = 4
SPLIT = 2
PIECES = ARRAYS * SPLIT
ROWS = 32
PER_TILE = TOK // ROWS
LINK = (BF16, BF16, BF16, F32, F32)
MOVE = ({"core": 3.2}, {"outer": 13.5}, {"outer": 6.8, "inner": 13.5}, {"x": 6.8}, {"x": 6.8})
WAIT = (1.0, 1.7, 2.4, 1.7, 2.4)
STATES_US, STEPS_US, INSIDE_US, CARRIED_US = 6.5, 2.0, 0.65, 0.5


def step_order(levels, tiles):
    free = {}
    clock = 0.0
    order, waiting, ready_tiles = [], [], []
    inside = 0
    landed = [0] * SPLIT
    share = tiles // SPLIT

    def send(level, kind, piece):
        end = clock
        for link, us in MOVE[level].items():
            free[link] = max(clock, free.get(link, 0.0)) + us / PIECES
            end = max(end, free[link])
        waiting.append((end + WAIT[level], len(order), kind, level, piece))

    def one_inside():
        nonlocal inside, clock
        order.append(("inside", 0, inside))
        inside += 1
        clock += INSIDE_US

    def one_carried():
        nonlocal clock
        tile = ready_tiles.pop(0)
        while inside <= tile:
            one_inside()
        order.append(("carried", 0, tile))
        clock += CARRIED_US

    for q in range(SPLIT):
        for a in range(ARRAYS):
            piece = SPLIT * a + q
            clock += STATES_US / PIECES / 2
            order.append(("state", 0, piece))
            send(0, "up", piece)
            clock += STATES_US / PIECES / 2
    while waiting:
        waiting.sort()
        ready = waiting[0][0]
        if ready_tiles and ready > clock + CARRIED_US:
            one_carried()
            continue
        if inside < tiles and ready > clock + INSIDE_US:
            one_inside()
            continue
        _, _, kind, level, piece = waiting.pop(0)
        if kind == "down" and level == 0:
            q = piece % SPLIT
            landed[q] += 1
            if landed[q] == ARRAYS:
                order.append(("landed", 0, q))
                ready_tiles.extend(range(q * share, (q + 1) * share))
            continue
        clock = max(clock, ready) + STEPS_US / PIECES
        if kind == "up" and level + 1 < levels:
            order.append(("up", level + 1, piece))
            send(level + 1, "up", piece)
        else:
            below = level if kind == "up" else level - 1
            order.append(("down", below, piece))
            send(below, "down", piece)
    while ready_tiles:
        one_carried()
    return order


def pair_rows(v):
    hi, lo = split2(v)
    return jnp.concatenate([hi, lo], axis=0)


def pair_lanes(v):
    hi, lo = split2(v)
    return jnp.concatenate([hi, lo], axis=1)


def layer_kernel(
    x_ref, g_ref, key_ref, query_ref, raw_ref, ld_ref, sb_ref, skip_ref, valid_ref,
    out_ref, pg_ref, kg_ref, qg_ref, sg_ref, val_ref,
    seg, seg_in, coef, own, got, snd, eown, egot, esnd, e_hi, e_lo,
    y_ref, dx_ref, ge_ref, ds_ref, dk_ref, dq_ref, sums_ref, part_a, part_b, part_c,
    up_send, up_recv, down_send, down_recv, log_send, log_recv,
    sum_send, sum_recv, *, levels, units, tiles, line, rows_of, groups
):
    me = lax.axis_index("seq")
    my_dp = lax.axis_index("dp")
    bits = [(me // (1 << b)) % 2 for b in range(levels)]
    peers = [me + (1 << b) * (1 - 2 * bits[b]) for b in range(levels)]
    half = [units >> (b + 1) for b in range(levels)]
    base = [0]
    for b in range(levels):
        base.append(base[b] + bits[b] * half[b])

    in_line = me % line
    my_line = me // line
    sum_peers = (
        [{"seq": my_line * line + (in_line + k) % line} for k in range(1, line)],
        [{"seq": (my_line + k) % rows_of * line + in_line} for k in range(1, rows_of)],
        [{"dp": (my_dp + k) % groups} for k in range(1, groups)],
    )
    sum_place = (in_line, my_line, my_dp)
    sum_size = (line, rows_of, groups)

    barrier = pltpu.get_barrier_semaphore()
    greeted = 0
    for group in sum_peers:
        for device in group:
            pl.semaphore_signal(barrier, inc=1, device_id=device, device_id_type=MESH)
            greeted += 1

    mask = valid_ref[0, 0].astype(F32)
    raw = raw_ref[...]
    logd = ld_ref[...]
    bias = sb_ref[...]
    heads = raw.shape[0]
    t = [timing(raw, logd, bias, mask, r) for r in (0, 1)]
    pick = iota((tiles, heads), 1)
    even = (pick == 2 * iota((tiles, heads), 0)).astype(F32)
    odd = (pick == 2 * iota((tiles, heads), 0) + 1).astype(F32)
    left_row = iota((tiles, LANES), 1) < LANES // 2
    for r in (0, 1):
        wide = jnp.broadcast_to(t[r]["total"], (heads, LANES))
        seg[0, r] = jnp.where(
            left_row, dot(even, wide, precision=HIGH), dot(odd, wide, precision=HIGH)
        )
    w = [parts_t(split2(t[r]["weight"])) for r in (0, 1)]
    e = [parts_t(split2(t[r]["decay"])) for r in (0, 1)]
    key = key_ref[...]
    query = query_ref[...]

    pl.semaphore_wait(barrier, greeted)

    def push(src, dst, send, recv, b):
        return pltpu.make_async_remote_copy(
            src_ref=src, dst_ref=dst, send_sem=send, recv_sem=recv,
            device_id={"seq": peers[b]}, device_id_type=MESH,
        )

    def up_copy(b, a):
        return push(snd[b].at[a], got[b].at[a], up_send.at[b, a], up_recv.at[b, a], b)

    def down_copy(b, a):
        if b == 0:
            dst = e_hi.at[a, pl.ds(bits[0] * half[0], half[0])]
        else:
            dst = egot[b].at[a]
        return push(esnd[b].at[a], dst, down_send.at[b, a], down_recv.at[b, a], b)

    def log_copy(b):
        return push(seg.at[b], seg_in.at[b], log_send.at[b], log_recv.at[b], b)

    def late_flag(b, a):
        late = (1 - bits[b]) if SCAN_LEFT[a] else bits[b]
        return late.astype(F32)

    def factors(b):
        log_copy(b).wait_recv()
        mine, other = seg[b], seg_in[b]
        if b + 2 < levels:
            seg[b + 1] = mine + other
            log_copy(b + 1).start()
        for a in range(ARRAYS):
            r = SCAN_DIR[a]
            late = late_flag(b, a)
            coef[b, a, 0] = jnp.exp((1.0 - late) * other[r])
            coef[b, a, 1] = jnp.exp(late * mine[r])
            coef[b, a, 2] = jnp.exp(late * other[r])
            coef[b, a, 3] = jnp.exp((1.0 - late) * mine[r])

    log_copy(0).start()

    key_t = key.astype(F32).T.astype(BF16)
    query_t = query.astype(F32).T.astype(BF16)
    key_tt = jnp.concatenate([key_t, key_t], axis=1)
    query_tt = jnp.concatenate([query_t, query_t], axis=1)
    half_tiles = tiles // 2
    piece_tiles = tiles // SPLIT
    keep_tiles = piece_tiles // 2
    scale = (w[0], e[1], w[1], e[0])

    def states(piece):
        a, q = piece // SPLIT, piece % SPLIT
        is_state = a % 2 == 0
        ref, lhs = (x_ref, key_tt) if is_state else (g_ref, query_tt)

        def state(at_tile):
            j = q * piece_tiles + at_tile
            lanes = pl.ds(pl.multiple_of(j * LANES, LANES), LANES)
            v = ref[:, lanes].astype(F32) * spread(scale[a], j)
            if not is_state:
                v = v * mask
            return dot(lhs, pair_rows(v)).reshape(PER_TILE, ROWS, LANES)

        def state_out(i, carry):
            u = state((1 - bits[0]) * keep_tiles + i)
            snd[0][piece, pl.ds(PER_TILE * i, PER_TILE)] = u.astype(snd[0].dtype)
            return carry

        def state_keep(i, carry):
            own[0][piece, pl.ds(PER_TILE * i, PER_TILE)] = state(bits[0] * keep_tiles + i)
            return carry

        lax.fori_loop(0, keep_tiles, state_out, 0, unroll=True)
        up_copy(0, piece).start()
        lax.fori_loop(0, keep_tiles, state_keep, 0, unroll=True)

    scores = dot(query, key, ((1,), (1,)))
    scores_t = dot(key, query, ((1,), (1,)))
    sign = (1.0, -1.0)
    at = [sign[r] * t[r]["place"] for r in (0, 1)]
    frm = [sign[r] * t[r]["place"] - jnp.log(t[r]["soft"]) for r in (0, 1)]

    at_cols = [parts_t(split3(v)) for v in at]
    frm_cols = [parts_t(split3(v)) for v in frm]
    rows_i, cols_i = iota((TOK, TOK), 0), iota((TOK, TOK), 1)
    lower, upper = rows_i >= cols_i, rows_i <= cols_i
    left = iota((TOK, LANES), 1) < LANES // 2
    ds_ref[...] = jnp.zeros_like(ds_ref)
    dk_ref[...] = jnp.zeros_like(dk_ref)
    dq_ref[...] = jnp.zeros_like(dq_ref)
    sums_ref[...] = jnp.zeros_like(sums_ref)
    head_row = iota((heads, TOK), 0)

    def row_of(v, h):
        return jnp.sum(jnp.where(head_row == h, v, 0.0), axis=0, keepdims=True)

    def head_ones(j):
        head = 2 * j + (iota((heads, LANES), 1) >= LANES // 2).astype(jnp.int32)
        return jnp.where(iota((heads, LANES), 0) == head, 1.0, 0.0).astype(BF16)

    def inside(j):
        lanes = pl.ds(pl.multiple_of(j * LANES, LANES), LANES)
        xb = x_ref[:, lanes]
        x = xb.astype(F32)
        g = g_ref[:, lanes].astype(F32) * mask
        zero = jnp.zeros_like(x)
        x_0, x_1 = jnp.where(left, x, zero).astype(BF16), jnp.where(left, zero, x).astype(BF16)
        g_0, g_1 = jnp.where(left, g, zero).astype(BF16), jnp.where(left, zero, g).astype(BF16)
        x_cat = jnp.concatenate([x_0, x_0, x_1, x_1], axis=0)
        g_cat = jnp.concatenate([g_0, g_0, g_1, g_1], axis=0)
        d_m = dot(jnp.concatenate([g_0, g_1], axis=0), xb, ((1,), (1,)))
        pick = iota((3 * heads, 2 * LANES), 0) % heads
        mine = 2 * j + (iota((3 * heads, 2 * LANES), 1) >= LANES).astype(jnp.int32)
        sel = jnp.where(pick == mine, 1.0, 0.0).astype(BF16)
        wsum = [0.0, 0.0]
        y, dx = [], []
        for r in (0, 1):
            at_b = dot(at_cols[r], sel)
            frm_b = dot(frm_cols[r], sel)
            m, m_t = [], []
            for k in (0, 1):
                at_row = row_of(at[r], 2 * j + k)
                frm_row = row_of(frm[r], 2 * j + k)
                cut = slice(k * LANES, (k + 1) * LANES)
                keep, keep_t = (lower, upper) if r == 0 else (upper, lower)
                wide = jnp.exp(jnp.where(keep, at_b[:, cut] - frm_row, -1e30))
                wide_t = jnp.exp(jnp.where(keep_t, at_row - frm_b[:, cut], -1e30))
                wsum[k] = wsum[k] + wide
                m += split2(wide * scores)
                m_t += split2(wide_t * scores_t)
            y.append(dot(jnp.concatenate(m, axis=1), x_cat))
            dx.append(dot(jnp.concatenate(m_t, axis=1), g_cat))
        ds_ref[...] += d_m[:TOK] * wsum[0] + d_m[TOK:] * wsum[1]
        y_ref[j] = y[0] + y[1]
        dx_ref[j] = dx[0] + dx[1]
        ones = head_ones(j)
        ones2 = jnp.concatenate([ones, ones], axis=1)
        quant = [x * dx[0], g * y[0] - x * dx[0], x * dx[1], g * y[1] - x * dx[1], g * x]
        for n, q in enumerate(quant):
            sums_ref[n] += dot(ones2, pair_lanes(q), ((1,), (1,)))

    def factor(b, a, which, unit):
        tile = (a % SPLIT) * piece_tiles + unit // PER_TILE
        return coef[b, a // SPLIT, which, pl.ds(tile, 1), :].reshape(1, 1, LANES)

    def each(count, most, fn):
        size = min(PER_TILE, most, count)
        if count == size:
            fn(0, size)
        else:
            lax.fori_loop(0, count // size, lambda i, c: (fn(i * size, size), c)[1], 0, unroll=2)

    def join(b, a):
        up_copy(b - 1, a).wait_recv()

        def joined(first, size):
            unit = base[b] + first
            mine = own[b - 1][a, pl.ds(first, size)]
            other = got[b - 1][a, pl.ds(first, size)].astype(F32)
            return factor(b - 1, a, 0, unit) * mine + factor(b - 1, a, 1, unit) * other

        def to_send(first, size):
            value = joined((1 - bits[b]) * half[b] + first, size)
            snd[b][a, pl.ds(first, size)] = value.astype(snd[b].dtype)

        def to_keep(first, size):
            own[b][a, pl.ds(first, size)] = joined(bits[b] * half[b] + first, size)

        each(half[b], PER_TILE, to_send)
        up_copy(b, a).start()
        each(half[b], PER_TILE, to_keep)

    def enter_down(b, a):
        late = late_flag(b, a // SPLIT)
        top = b == levels - 1
        if top:
            up_copy(b, a).wait_recv()
        else:
            down_copy(b + 1, a).wait_recv()

        def entering(first, size, where):
            if where == "own":
                return eown[b + 1][a, pl.ds(first, size)]
            return egot[b + 1][a, pl.ds(first, size)].astype(F32)

        def for_peer(first, size, at_unit, where):
            value = (1.0 - late) * own[b][a, pl.ds(at_unit, size)]
            if where is not None:
                value += factor(b, a, 3, base[b + 1] + at_unit) * entering(first, size, where)
            esnd[b][a, pl.ds(at_unit, size)] = value.astype(esnd[b].dtype)

        def for_me(first, size, at_unit, where):
            value = late * got[b][a, pl.ds(at_unit, size)].astype(F32)
            if where is not None:
                value += factor(b, a, 2, base[b + 1] + at_unit) * entering(first, size, where)
            if b == 0:
                hi, lo = split2(value)
                e_hi[a, pl.ds(bits[0] * half[0] + at_unit, size)] = hi
                e_lo[a, pl.ds(bits[0] * half[0] + at_unit, size)] = lo
                e_lo[a, pl.ds((1 - bits[0]) * half[0] + at_unit, size)] = jnp.zeros_like(lo)
            else:
                eown[b][a, pl.ds(at_unit, size)] = value

        def sweep(fn):
            if top:
                each(half[b], PER_TILE, lambda first, size: fn(first, size, first, None))
                return
            h = half[b + 1]
            for where, start in (("own", bits[b + 1] * h), ("got", (1 - bits[b + 1]) * h)):
                each(h, PER_TILE, lambda f, n, where=where, start=start: fn(f, n, start + f, where))

        sweep(for_peer)
        down_copy(b, a).start()
        sweep(for_me)

    skip2 = parts_t(split2(jnp.broadcast_to(column(skip_ref[...]), (heads, TOK))))
    query2 = jnp.concatenate([query, query], axis=1)
    key2 = jnp.concatenate([key, key], axis=1)

    def entered(a, j):
        piece = SPLIT * a + j // piece_tiles
        tile = pl.ds(PER_TILE * (j % piece_tiles), PER_TILE)
        return e_hi[piece, tile].reshape(TOK, LANES), e_lo[piece, tile].reshape(TOK, LANES)

    def carried(j):
        lanes = pl.ds(pl.multiple_of(j * LANES, LANES), LANES)
        x = x_ref[:, lanes].astype(F32)
        g = g_ref[:, lanes].astype(F32) * mask
        ones = head_ones(j)
        ones2 = jnp.concatenate([ones, ones], axis=1)
        y, dx = y_ref[j], dx_ref[j]
        for r, (a_in, a_back) in enumerate(((0, 3), (2, 1))):
            e_in, e_back = entered(a_in, j), entered(a_back, j)
            y_more = spread(e[r], j) * dot(query2, jnp.concatenate(e_in, axis=0))
            dx_more = spread(w[r], j) * dot(key2, jnp.concatenate(e_back, axis=0))
            sums_ref[5 + 2 * r] += dot(ones2, pair_lanes(g * y_more), ((1,), (1,)))
            sums_ref[6 + 2 * r] += dot(ones2, pair_lanes(x * dx_more), ((1,), (1,)))
            through = (e_in[0].astype(F32) + e_in[1].astype(F32)) * (
                e_back[0].astype(F32) + e_back[1].astype(F32)
            )
            ge_ref[r, :, lanes] = jnp.sum(through.reshape(TOK // 8, 8, LANES), axis=0)
            y, dx = y + y_more, dx + dx_more
        skip_b = spread(skip2, j)
        out_ref[:, lanes] = (mask * (y + skip_b * x)).astype(BF16)
        pg_ref[:, lanes] = (dx + skip_b * g).astype(BF16)

    factored, made = 0, 0
    for kind, level, n in step_order(levels, tiles):
        if kind == "state":
            states(n)
            made += 1
            if made % SPLIT == 0 and factored < levels - 1:
                factors(factored)
                factored += 1
        elif kind == "up":
            while factored < min(level + 1, levels - 1):
                factors(factored)
                factored += 1
            join(level, n)
        elif kind == "down":
            while factored < levels - 1:
                factors(factored)
                factored += 1
            enter_down(level, n)
        elif kind == "landed":
            for a in range(ARRAYS):
                down_copy(0, SPLIT * a + n).wait_recv()
        elif kind == "inside":
            inside(n)
        else:
            carried(n)

    def projections(j):
        lanes = pl.ds(pl.multiple_of(j * LANES, LANES), LANES)
        x = x_ref[:, lanes].astype(F32)
        g = g_ref[:, lanes].astype(F32) * mask
        left_sides, right_sides = ([], []), ([], [])
        for r, (a_in, a_back) in enumerate(((0, 3), (2, 1))):
            hi, _ = entered(a_back, j)
            left_sides[0].append(pair_lanes(x * spread(w[r], j)))
            right_sides[0].extend([hi, hi])
            hi, _ = entered(a_in, j)
            left_sides[1].append(pair_lanes(g * spread(e[r], j)))
            right_sides[1].extend([hi, hi])
        for n, acc in enumerate((dk_ref, dq_ref)):
            acc[...] += dot(
                jnp.concatenate(left_sides[n], axis=1),
                jnp.concatenate(right_sides[n], axis=1),
                ((1,), (1,)),
            )

    projected = [0]

    def project_some(stop):
        if stop > projected[0]:
            lax.fori_loop(projected[0], stop, lambda i, c: (projections(i), c)[1], 0)
        projected[0] = stop

    width = tiles * LANES
    all_ones = jnp.where(
        iota((heads, width), 0) == iota((heads, width), 1) // (LANES // 2), 1.0, 0.0
    ).astype(BF16)
    upto = (rows_i <= cols_i).astype(F32)
    since = (rows_i >= cols_i).astype(F32)
    ones_row = jnp.ones((8, TOK), F32)

    def total_row(v):
        return dot(ones_row, v, ((1,), (1,)), precision=HIGH)[0:1]

    step_grad = jnp.zeros((heads, TOK), F32)
    decay_rows, bias_rows = [], []
    for r in (0, 1):
        hi, lo = split2(ge_ref[r])
        passing = jnp.sum(
            dot(all_ones, hi, ((1,), (1,))) + dot(all_ones, lo, ((1,), (1,))),
            axis=1, keepdims=True,
        )
        col_in, net_in = sums_ref[2 * r], sums_ref[2 * r + 1]
        row_more, col_more = sums_ref[5 + 2 * r], sums_ref[6 + 2 * r]
        flow = jnp.exp(t[r]["total"]) * passing + jnp.sum(col_more, axis=1, keepdims=True)
        net = net_in + row_more - col_more
        d_log = flow + dot(net, since if r == 0 else upto, precision=HIGH)
        slope = t[r]["slope"] * mask
        raw_grad = (col_in + col_more) * (slope / t[r]["soft"]) + t[r]["rate"] * d_log * slope
        step_grad += raw_grad
        decay_rows.append(-jnp.exp(logd[r : r + 1, :]) * total_row(t[r]["steps"] * d_log))
        bias_rows.append(total_row(raw_grad))
    sg_ref[...] = step_grad

    skip_row = total_row(sums_ref[4])
    value = jnp.concatenate(
        [
            jnp.concatenate(decay_rows + bias_rows, axis=1),
            jnp.concatenate([skip_row] * 4, axis=1),
        ],
        axis=0,
    )
    for n, part in enumerate((part_a, part_b, part_c)):
        place, size = sum_place[n], sum_size[n]
        part[place] = value
        for k in range(1, size):
            pltpu.make_async_remote_copy(
                src_ref=part.at[place], dst_ref=part.at[place],
                send_sem=sum_send.at[n, k], recv_sem=sum_recv.at[n, place],
                device_id=sum_peers[n][k - 1], device_id_type=MESH,
            ).start()
        project_some((tiles // 3, 2 * tiles // 3, tiles)[n])
        for k in range(1, size):
            other = (place + k) % size
            pltpu.make_async_remote_copy(
                src_ref=part.at[other], dst_ref=part.at[other],
                send_sem=sum_send.at[n, k], recv_sem=sum_recv.at[n, other],
                device_id=sum_peers[n][k - 1], device_id_type=MESH,
            ).wait_recv()
        value = part[0]
        for k in range(1, size):
            value += part[k]
    ds_hi, ds_lo = split2(ds_ref[...])
    qg_ref[...] = dq_ref[...] + dot(
        jnp.concatenate([ds_hi, ds_lo], axis=1), jnp.concatenate([key, key], axis=0)
    )
    kg_ref[...] = (
        dk_ref[...] + dot(ds_hi, query, ((0,), (0,))) + dot(ds_lo, query, ((0,), (0,)))
    )
    val_ref[...] = value

    for b in range(levels):
        if b + 1 < levels:
            log_copy(b).wait_send()
        for a in range(PIECES):
            up_copy(b, a).wait_send()
            down_copy(b, a).wait_send()
    for n, part in enumerate((part_a, part_b, part_c)):
        for k in range(1, sum_size[n]):
            pltpu.make_async_remote_copy(
                src_ref=part.at[sum_place[n]], dst_ref=part.at[sum_place[n]],
                send_sem=sum_send.at[n, k], recv_sem=sum_recv.at[n, sum_place[n]],
                device_id=sum_peers[n][k - 1], device_id_type=MESH,
            ).wait_send()


def finish_kernel(*refs):
    for source, target in zip(refs[:5], refs[6:11]):
        target[...] = source[...]
    value = refs[5][...]
    dec_ref, bias_ref, skipg_ref = refs[11:]
    heads = dec_ref.shape[1]
    for r in (0, 1):
        dec_ref[r : r + 1, :] = value[0:1, r * heads : (r + 1) * heads]
        bias_ref[r : r + 1, :] = value[0:1, (2 + r) * heads : (3 + r) * heads]
    skipg_ref[...] = value[1:2, :heads]


def body(
    patches, key_proj, query_proj, step_raw, log_decay, step_bias, skip_gain, group_valid, out_grad
):
    heads = step_raw.shape[1]
    width = patches.shape[2]
    tiles = width // LANES
    units = tiles // SPLIT * PER_TILE
    seq = lax.axis_size("seq")
    groups = lax.axis_size("dp")
    levels = seq.bit_length() - 1
    line = min(8, seq)
    rows_of = seq // line
    vmem = pl.BlockSpec(memory_space=pltpu.VMEM)
    h = [units >> (b + 1) for b in range(levels)]
    unit = (ROWS, LANES)
    link = [LINK[b] for b in range(levels)]

    def blocks(dtypes):
        return [pltpu.VMEM((PIECES, h[b]) + unit, dtypes[b]) for b in range(levels)]

    wide = [F32] * levels
    dma = pltpu.SemaphoreType.DMA
    size = max(line, rows_of, groups)
    made = (
        pl.pallas_call(
            functools.partial(
                layer_kernel, levels=levels, units=units, tiles=tiles,
                line=line, rows_of=rows_of, groups=groups,
            ),
            out_shape=(
                jax.ShapeDtypeStruct((TOK, width), BF16),
                jax.ShapeDtypeStruct((TOK, width), BF16),
                jax.ShapeDtypeStruct((TOK, LANES), F32),
                jax.ShapeDtypeStruct((TOK, LANES), F32),
                jax.ShapeDtypeStruct((heads, TOK), F32),
                jax.ShapeDtypeStruct((2, LANES), F32),
            ),
            in_specs=[vmem] * 8 + [pl.BlockSpec(memory_space=pltpu.SMEM)],
            out_specs=(vmem,) * 6,
            scratch_shapes=[
                pltpu.VMEM((levels, 2, tiles, LANES), F32),
                pltpu.VMEM((levels, 2, tiles, LANES), F32),
                pltpu.VMEM((levels, 4, 4, tiles, LANES), F32),
                blocks(wide),
                blocks(link),
                blocks(link),
                blocks(wide),
                blocks(link),
                blocks(link),
                pltpu.VMEM((PIECES, units) + unit, BF16),
                pltpu.VMEM((PIECES, units) + unit, BF16),
                pltpu.VMEM((tiles, TOK, LANES), F32),
                pltpu.VMEM((tiles, TOK, LANES), F32),
                pltpu.VMEM((2, 8, width), F32),
                pltpu.VMEM((TOK, TOK), F32),
                pltpu.VMEM((TOK, LANES), F32),
                pltpu.VMEM((TOK, LANES), F32),
                pltpu.VMEM((9, heads, TOK), F32),
                pltpu.VMEM((line, 2, LANES), F32),
                pltpu.VMEM((rows_of, 2, LANES), F32),
                pltpu.VMEM((groups, 2, LANES), F32),
                dma((levels, PIECES)),
                dma((levels, PIECES)),
                dma((levels, PIECES)),
                dma((levels, PIECES)),
                dma((levels,)),
                dma((levels,)),
                dma((3, size)),
                dma((3, size)),
            ],
            compiler_params=pltpu.CompilerParams(collective_id=0, has_side_effects=True),
            name="layer",
        )(
            patches[0], out_grad[0], key_proj[0], query_proj[0], step_raw[0],
            log_decay, step_bias, skip_gain[None], group_valid,
        )
    )
    output, patch_grad, key_grad, query_grad, step_grad, decay_grad, bias_grad, skip_grad = (
        pl.pallas_call(
            finish_kernel,
            out_shape=tuple(jax.ShapeDtypeStruct(m.shape, m.dtype) for m in made[:5])
            + (
                jax.ShapeDtypeStruct((2, heads), F32),
                jax.ShapeDtypeStruct((2, heads), F32),
                jax.ShapeDtypeStruct((1, heads), F32),
            ),
            in_specs=[vmem] * 6,
            out_specs=(vmem,) * 8,
            name="finish",
        )(*made)
    )
    return (
        output[None],
        patch_grad[None],
        key_grad[None],
        query_grad[None],
        step_grad[None],
        decay_grad,
        bias_grad,
        skip_grad[0],
    )


def solution(mesh):
    in_specs = (
        P("dp", "seq", None),
        P("dp", "seq", None),
        P("dp", "seq", None),
        P("dp", None, "seq"),
        P(),
        P(),
        P(),
        P("dp", "seq"),
        P("dp", "seq", None),
    )
    out_specs = (
        P("dp", "seq", None),
        P("dp", "seq", None),
        P("dp", "seq", None),
        P("dp", "seq", None),
        P("dp", None, "seq"),
        P(),
        P(),
        P(),
    )
    return jax.shard_map(body, mesh=mesh, in_specs=in_specs, out_specs=out_specs, check_vma=False)
```

time: 112 us -> 92.1 us (0.82)
  Pallas kernels: 103 us -> 90.5 us
  local copies, waits for them, and re-layouts: 6.8 us -> 0 us
    pallas_call x1, Pallas kernels: 103 us -> 88.2 us  [body(): pl.pallas_call(functools.partial(layer_kernel, levels=levels, units=units...]
    unnamed x22 -> x0, local copies, waits for them, and re-layouts: 6.8 us -> none
    pallas_call x0 -> x1, Pallas kernels: none -> 2.27 us  [body(): pl.pallas_call(finish_kernel, out_shape=tuple((jax.ShapeDtypeStruct(m.sha...]
where the time goes in v2:
time: 92.1 us; the launch traced here: 91.9 us
  Pallas kernels  90.5 us (98%)
  between operations  1.44 us (2%)
    pallas_call x1, Pallas kernels, body(): pl.pallas_call(functools.partial(layer_kernel, levels=levels, units=units...  88.2 us
    pallas_call x1, Pallas kernels, body(): pl.pallas_call(finish_kernel, out_shape=tuple((jax.ShapeDtypeStruct(m.sha...  2.27 us

profile of v2, /device:TPU:1, one launch (start us, length us, event | category | flops | bytes accessed | tf_op | source)
XLA Modules:
  0.0 91.9 jit_solution(7990110189250278359)
XLA Ops:
  1.3 88.2 %layer.1 = (bf16[128,2048]{1,0:T(8,128)(2,1)}, bf16[128,2048]{1,0:T(8,128)(2,1)}, f32[128,128]{1,0:T(8,128)}, f32[128,128]{1,0:T(8,128)}, f32[32,128]{1,0:T(8,128)}, /*index=5*/f32[2,128]{1,0:T(2,128)}) custom-call(bf16[128,2048]{1,0:T(8,128)(2,1)} %bitcast.12, bf16[128,2048]{1,0:T(8,128)(2,1)} %bitcast.13, bf16[128,128]{1,0:T(8,128)(2,1)} %bitcast.14, ...), custom_call_target="tpu_custom_call" | custom-call | tf_op jit(solution)/shard_map/layer/pallas_call | solution.py:652
  89.5 2.3 %finish.1 = (bf16[128,2048]{1,0:T(8,128)(2,1)}, bf16[128,2048]{1,0:T(8,128)(2,1)}, f32[128,128]{1,0:T(8,128)}, f32[128,128]{1,0:T(8,128)}, f32[32,128]{1,0:T(8,1...) custom-call(bf16[128,2048]{1,0:T(8,128)(2,1)} %get-tuple-element.22.refs_0_, ...), custom_call_target="tpu_custom_call" | custom-call | tf_op jit(solution)/shard_map/finish/pallas_call | solution.py:706

commit v3 on v2

--- a/solution.py
+++ b/solution.py
@@ -12,16 +12,13 @@
 MESH = pl.DeviceIdType.MESH
 TOK = 128
 LANES = 128
-HIGH = lax.Precision.HIGHEST
 
 SCAN_DIR = (0, 1, 1, 0)
 SCAN_LEFT = (False, False, True, True)
 
 
-def dot(a, b, dims=((1,), (0,)), precision=None):
-    return lax.dot_general(
-        a, b, (dims, ((), ())), precision=precision, preferred_element_type=F32
-    )
+def dot(a, b, dims=((1,), (0,))):
+    return lax.dot_general(a, b, (dims, ((), ())), preferred_element_type=F32)
 
 
 def iota(shape, axis):
@@ -63,8 +60,8 @@
     slope = 1.0 / (1.0 + jnp.exp(-shifted))
     steps = soft * mask
     logs = steps * rate
-    upto = (iota((TOK, TOK), 0) <= iota((TOK, TOK), 1)).astype(F32)
-    cum = dot(logs, upto, precision=HIGH)
+    upto = (iota((TOK, TOK), 0) <= iota((TOK, TOK), 1)).astype(F32).astype(BF16)
+    cum = dot(jnp.concatenate(split3(logs), axis=1), jnp.concatenate([upto] * 3, axis=0))
     total = cum[:, TOK - 1 :]
     if r == 0:
         place = cum
@@ -97,8 +94,8 @@
 ROWS = 32
 PER_TILE = TOK // ROWS
 LINK = (BF16, BF16, BF16, F32, F32)
-MOVE = ({"core": 3.2}, {"outer": 13.5}, {"outer": 6.8, "inner": 13.5}, {"x": 6.8}, {"x": 6.8})
-WAIT = (1.0, 1.7, 2.4, 1.7, 2.4)
+MOVE = ({"core": 2.5}, {"outer": 10.5}, {"outer": 5.2, "inner": 10.5}, {"x": 5.0}, {"x": 5.0})
+WAIT = (1.5, 3.0, 4.0, 3.0, 4.0)
 STATES_US, STEPS_US, INSIDE_US, CARRIED_US = 6.5, 2.0, 0.65, 0.5
 
 
@@ -107,8 +104,9 @@
     clock = 0.0
     order, waiting, ready_tiles = [], [], []
     inside = 0
-    landed = [0] * SPLIT
+    sent, landed = [0] * SPLIT, [0] * SPLIT
     share = tiles // SPLIT
+    states = [SPLIT * a + q for q in range(SPLIT) for a in range(ARRAYS)]
 
     def send(level, kind, piece):
         end = clock
@@ -125,22 +123,22 @@
 
     def one_carried():
         nonlocal clock
-        tile = ready_tiles.pop(0)
-        while inside <= tile:
+        kind, q, i = ready_tiles.pop(0)
+        while inside < (q + 1) * share:
             one_inside()
-        order.append(("carried", 0, tile))
+        order.append((kind, q, i))
         clock += CARRIED_US
 
-    for q in range(SPLIT):
-        for a in range(ARRAYS):
-            piece = SPLIT * a + q
+    while waiting or states:
+        waiting.sort()
+        ready = waiting[0][0] if waiting else float("inf")
+        if states and ready > clock:
+            piece = states.pop(0)
             clock += STATES_US / PIECES / 2
             order.append(("state", 0, piece))
             send(0, "up", piece)
             clock += STATES_US / PIECES / 2
-    while waiting:
-        waiting.sort()
-        ready = waiting[0][0]
+            continue
         if ready_tiles and ready > clock + CARRIED_US:
             one_carried()
             continue
@@ -152,8 +150,8 @@
             q = piece % SPLIT
             landed[q] += 1
             if landed[q] == ARRAYS:
-                order.append(("landed", 0, q))
-                ready_tiles.extend(range(q * share, (q + 1) * share))
+                order.append(("landed", q, q))
+                ready_tiles.extend(("other", q, i) for i in range(share // 2))
             continue
         clock = max(clock, ready) + STEPS_US / PIECES
         if kind == "up" and level + 1 < levels:
@@ -163,6 +161,11 @@
             below = level if kind == "up" else level - 1
             order.append(("down", below, piece))
             send(below, "down", piece)
+            if below == 0:
+                q = piece % SPLIT
+                sent[q] += 1
+                if sent[q] == ARRAYS:
+                    ready_tiles.extend(("own", q, i) for i in range(share // 2))
     while ready_tiles:
         one_carried()
     return order
@@ -179,12 +182,12 @@
 
 
 def layer_kernel(
-    x_ref, g_ref, key_ref, query_ref, raw_ref, ld_ref, sb_ref, skip_ref, valid_ref,
-    out_ref, pg_ref, kg_ref, qg_ref, sg_ref, val_ref,
-    seg, seg_in, coef, own, got, snd, eown, egot, esnd, e_hi, e_lo,
+    x_hbm, g_hbm, key_ref, query_ref, raw_ref, ld_ref, sb_ref, skip_ref, valid_ref,
+    out_hbm, pg_hbm, kg_ref, qg_ref, sg_ref, val_ref,
+    x_ref, g_ref, out_ref, pg_ref, seg, seg_in, coef, own, got, snd, eown, egot, esnd, e_hi, e_lo,
     y_ref, dx_ref, ge_ref, ds_ref, dk_ref, dq_ref, sums_ref, part_a, part_b, part_c,
     up_send, up_recv, down_send, down_recv, log_send, log_recv,
-    sum_send, sum_recv, *, levels, units, tiles, line, rows_of, groups
+    sum_send, sum_recv, load_sem, store_sem, *, levels, units, tiles, line, rows_of, groups
 ):
     me = lax.axis_index("seq")
     my_dp = lax.axis_index("dp")
@@ -205,6 +208,13 @@
     sum_place = (in_line, my_line, my_dp)
     sum_size = (line, rows_of, groups)
 
+    loads = [
+        pltpu.make_async_copy(x_hbm, x_ref, load_sem.at[0]),
+        pltpu.make_async_copy(g_hbm, g_ref, load_sem.at[1]),
+    ]
+    for load in loads:
+        load.start()
+
     barrier = pltpu.get_barrier_semaphore()
     greeted = 0
     for group in sum_peers:
@@ -218,15 +228,15 @@
     bias = sb_ref[...]
     heads = raw.shape[0]
     t = [timing(raw, logd, bias, mask, r) for r in (0, 1)]
-    pick = iota((tiles, heads), 1)
-    even = (pick == 2 * iota((tiles, heads), 0)).astype(F32)
-    odd = (pick == 2 * iota((tiles, heads), 0) + 1).astype(F32)
+    pick_row = iota((2 * tiles, 3 * heads), 0)
+    pick_head = jnp.where(pick_row < tiles, 2 * pick_row, 2 * (pick_row - tiles) + 1)
+    picks = iota((2 * tiles, 3 * heads), 1) % heads == pick_head
+    picks = jnp.where(picks, 1.0, 0.0).astype(BF16)
     left_row = iota((tiles, LANES), 1) < LANES // 2
     for r in (0, 1):
-        wide = jnp.broadcast_to(t[r]["total"], (heads, LANES))
-        seg[0, r] = jnp.where(
-            left_row, dot(even, wide, precision=HIGH), dot(odd, wide, precision=HIGH)
-        )
+        parts = [p.astype(F32) for p in split3(jnp.broadcast_to(t[r]["total"], (heads, LANES)))]
+        rows = dot(picks, jnp.concatenate(parts, axis=0).astype(BF16))
+        seg[0, r] = jnp.where(left_row, rows[:tiles], rows[tiles:])
     w = [parts_t(split2(t[r]["weight"])) for r in (0, 1)]
     e = [parts_t(split2(t[r]["decay"])) for r in (0, 1)]
     key = key_ref[...]
@@ -272,6 +282,8 @@
             coef[b, a, 3] = jnp.exp((1.0 - late) * mine[r])
 
     log_copy(0).start()
+    for load in loads:
+        load.wait()
 
     key_t = key.astype(F32).T.astype(BF16)
     query_t = query.astype(F32).T.astype(BF16)
@@ -323,6 +335,7 @@
     dk_ref[...] = jnp.zeros_like(dk_ref)
     dq_ref[...] = jnp.zeros_like(dq_ref)
     sums_ref[...] = jnp.zeros_like(sums_ref)
+    ge_ref[...] = jnp.zeros_like(ge_ref)
     head_row = iota((heads, TOK), 0)
 
     def row_of(v, h):
@@ -472,11 +485,11 @@
             through = (e_in[0].astype(F32) + e_in[1].astype(F32)) * (
                 e_back[0].astype(F32) + e_back[1].astype(F32)
             )
-            ge_ref[r, :, lanes] = jnp.sum(through.reshape(TOK // 8, 8, LANES), axis=0)
+            through = jnp.sum(through.reshape(TOK // 8, 8, LANES), axis=0)
+            ge_ref[r] += dot(ones2, pair_lanes(through), ((1,), (1,)))
             y, dx = y + y_more, dx + dx_more
-        skip_b = spread(skip2, j)
-        out_ref[:, lanes] = (mask * (y + skip_b * x)).astype(BF16)
-        pg_ref[:, lanes] = (dx + skip_b * g).astype(BF16)
+        y_ref[j] = y
+        dx_ref[j] = dx
 
     factored, made = 0, 0
     for kind, level, n in step_order(levels, tiles):
@@ -502,12 +515,16 @@
         elif kind == "inside":
             inside(n)
         else:
-            carried(n)
+            bit = bits[0] if kind == "own" else 1 - bits[0]
+            carried(level * piece_tiles + bit * keep_tiles + n)
 
     def projections(j):
         lanes = pl.ds(pl.multiple_of(j * LANES, LANES), LANES)
         x = x_ref[:, lanes].astype(F32)
         g = g_ref[:, lanes].astype(F32) * mask
+        skip_b = spread(skip2, j)
+        out_ref[:, lanes] = (mask * (y_ref[j] + skip_b * x)).astype(BF16)
+        pg_ref[:, lanes] = (dx_ref[j] + skip_b * g).astype(BF16)
         left_sides, right_sides = ([], []), ([], [])
         for r, (a_in, a_back) in enumerate(((0, 3), (2, 1))):
             hi, _ = entered(a_back, j)
@@ -523,6 +540,10 @@
                 ((1,), (1,)),
             )
 
+    stores = [
+        pltpu.make_async_copy(out_ref, out_hbm, store_sem.at[0]),
+        pltpu.make_async_copy(pg_ref, pg_hbm, store_sem.at[1]),
+    ]
     projected = [0]
 
     def project_some(stop):
@@ -530,42 +551,35 @@
             lax.fori_loop(projected[0], stop, lambda i, c: (projections(i), c)[1], 0)
         projected[0] = stop
 
-    width = tiles * LANES
-    all_ones = jnp.where(
-        iota((heads, width), 0) == iota((heads, width), 1) // (LANES // 2), 1.0, 0.0
-    ).astype(BF16)
-    upto = (rows_i <= cols_i).astype(F32)
-    since = (rows_i >= cols_i).astype(F32)
-    ones_row = jnp.ones((8, TOK), F32)
-
-    def total_row(v):
-        return dot(ones_row, v, ((1,), (1,)), precision=HIGH)[0:1]
-
+    upto = jnp.where(rows_i <= cols_i, 1.0, 0.0).astype(BF16)
+    since = jnp.where(rows_i >= cols_i, 1.0, 0.0).astype(BF16)
     step_grad = jnp.zeros((heads, TOK), F32)
-    decay_rows, bias_rows = [], []
+    rates = [-jnp.exp(logd[r : r + 1, :]) for r in (0, 1)]
+    by_decay, by_bias = [], []
     for r in (0, 1):
-        hi, lo = split2(ge_ref[r])
-        passing = jnp.sum(
-            dot(all_ones, hi, ((1,), (1,))) + dot(all_ones, lo, ((1,), (1,))),
-            axis=1, keepdims=True,
-        )
+        passing = jnp.sum(ge_ref[r], axis=1, keepdims=True)
         col_in, net_in = sums_ref[2 * r], sums_ref[2 * r + 1]
         row_more, col_more = sums_ref[5 + 2 * r], sums_ref[6 + 2 * r]
         flow = jnp.exp(t[r]["total"]) * passing + jnp.sum(col_more, axis=1, keepdims=True)
         net = net_in + row_more - col_more
-        d_log = flow + dot(net, since if r == 0 else upto, precision=HIGH)
+        over = since if r == 0 else upto
+        d_log = flow + dot(pair_lanes(net), jnp.concatenate([over, over], axis=0))
         slope = t[r]["slope"] * mask
         raw_grad = (col_in + col_more) * (slope / t[r]["soft"]) + t[r]["rate"] * d_log * slope
         step_grad += raw_grad
-        decay_rows.append(-jnp.exp(logd[r : r + 1, :]) * total_row(t[r]["steps"] * d_log))
-        bias_rows.append(total_row(raw_grad))
+        by_decay.append(t[r]["steps"] * d_log)
+        by_bias.append(raw_grad)
     sg_ref[...] = step_grad
 
-    skip_row = total_row(sums_ref[4])
+    summed = jnp.concatenate(by_decay + by_bias + [sums_ref[4]], axis=0)
+    totals = dot(jnp.ones((8, 2 * TOK), BF16), pair_lanes(summed), ((1,), (1,)))[0:1]
     value = jnp.concatenate(
         [
-            jnp.concatenate(decay_rows + bias_rows, axis=1),
-            jnp.concatenate([skip_row] * 4, axis=1),
+            jnp.concatenate(
+                [rates[0] * totals[:, :heads], rates[1] * totals[:, heads : 2 * heads],
+                 totals[:, 2 * heads : 4 * heads]], axis=1,
+            ),
+            jnp.concatenate([totals[:, 4 * heads :]] * 4, axis=1),
         ],
         axis=0,
     )
@@ -578,7 +592,10 @@
                 send_sem=sum_send.at[n, k], recv_sem=sum_recv.at[n, place],
                 device_id=sum_peers[n][k - 1], device_id_type=MESH,
             ).start()
-        project_some((tiles // 3, 2 * tiles // 3, tiles)[n])
+        project_some((tiles // 2, tiles, tiles)[n])
+        if n == 1:
+            for store in stores:
+                store.start()
         for k in range(1, size):
             other = (place + k) % size
             pltpu.make_async_remote_copy(
@@ -597,6 +614,8 @@
         dk_ref[...] + dot(ds_hi, query, ((0,), (0,))) + dot(ds_lo, query, ((0,), (0,)))
     )
     val_ref[...] = value
+    for store in stores:
+        store.wait()
 
     for b in range(levels):
         if b + 1 < levels:
@@ -662,9 +681,13 @@
                 jax.ShapeDtypeStruct((heads, TOK), F32),
                 jax.ShapeDtypeStruct((2, LANES), F32),
             ),
-            in_specs=[vmem] * 8 + [pl.BlockSpec(memory_space=pltpu.SMEM)],
-            out_specs=(vmem,) * 6,
+            in_specs=[pl.BlockSpec(memory_space=pl.ANY)] * 2 + [vmem] * 6 + [pl.BlockSpec(memory_space=pltpu.SMEM)],
+            out_specs=(pl.BlockSpec(memory_space=pl.ANY),) * 2 + (vmem,) * 4,
             scratch_shapes=[
+                pltpu.VMEM((TOK, width), BF16),
+                pltpu.VMEM((TOK, width), BF16),
+                pltpu.VMEM((TOK, width), BF16),
+                pltpu.VMEM((TOK, width), BF16),
                 pltpu.VMEM((levels, 2, tiles, LANES), F32),
                 pltpu.VMEM((levels, 2, tiles, LANES), F32),
                 pltpu.VMEM((levels, 4, 4, tiles, LANES), F32),
@@ -678,7 +701,7 @@
                 pltpu.VMEM((PIECES, units) + unit, BF16),
                 pltpu.VMEM((tiles, TOK, LANES), F32),
                 pltpu.VMEM((tiles, TOK, LANES), F32),
-                pltpu.VMEM((2, 8, width), F32),
+                pltpu.VMEM((2, heads, 8), F32),
                 pltpu.VMEM((TOK, TOK), F32),
                 pltpu.VMEM((TOK, LANES), F32),
                 pltpu.VMEM((TOK, LANES), F32),
@@ -694,6 +717,8 @@
                 dma((levels,)),
                 dma((3, size)),
                 dma((3, size)),
+                dma((2,)),
+                dma((2,)),
             ],
             compiler_params=pltpu.CompilerParams(collective_id=0, has_side_effects=True),
             name="layer",

time: 92.1 us -> 86.5 us (0.939)
  Pallas kernels: 90.5 us -> 84.9 us
    pallas_call x1, Pallas kernels: 88.2 us -> 82.6 us  [body(): pl.pallas_call(functools.partial(layer_kernel, levels=levels, units=units...]
where the time goes in v3:
time: 86.5 us; the launch traced here: 86.3 us
  Pallas kernels  84.9 us (98%)
  between operations  1.44 us (2%)
    pallas_call x1, Pallas kernels, body(): pl.pallas_call(functools.partial(layer_kernel, levels=levels, units=units...  82.6 us
    pallas_call x1, Pallas kernels, body(): pl.pallas_call(finish_kernel, out_shape=tuple((jax.ShapeDtypeStruct(m.sha...  2.27 us

profile of v3, /device:TPU:1, one launch (start us, length us, event | category | flops | bytes accessed | tf_op | source)
XLA Modules:
  0.0 86.3 jit_solution(8548932129576728059)
XLA Ops:
  1.3 82.6 %layer.1 = (bf16[128,2048]{1,0:T(8,128)(2,1)}, bf16[128,2048]{1,0:T(8,128)(2,1)}, f32[128,128]{1,0:T(8,128)}, f32[128,128]{1,0:T(8,128)}, f32[32,128]{1,0:T(8,128)}, /*index=5*/f32[2,128]{1,0:T(2,128)}) custom-call(bf16[128,2048]{1,0:T(8,128)(2,1)} %bitcast.12, bf16[128,2048]{1,0:T(8,128)(2,1)} %bitcast.13, bf16[128,128]{1,0:T(8,128)(2,1)} %bitcast.14, ...), custom_call_target="tpu_custom_call" | custom-call | tf_op jit(solution)/shard_map/layer/pallas_call | solution.py:671
  83.9 2.3 %finish.1 = (bf16[128,2048]{1,0:T(8,128)(2,1)}, bf16[128,2048]{1,0:T(8,128)(2,1)}, f32[128,128]{1,0:T(8,128)}, f32[128,128]{1,0:T(8,128)}, f32[32,128]{1,0:T(8,1...) custom-call(bf16[128,2048]{1,0:T(8,128)(2,1)} %get-tuple-element.22.refs_0_, ...), custom_call_target="tpu_custom_call" | custom-call | tf_op jit(solution)/shard_map/finish/pallas_call | solution.py:731
